TPU v7x, 32 devices: a whole 2x2x4 slice. The times are simulated.
32 devices in a mesh: groups: 2 (over y), patch: 8 (over z, x), batch: 2 (over core).
Axes of the slice: x: 2, y: 2, z: 4, core: 2. Of those that a mesh axis runs over, the one named last changes fastest.
Arguments:
- subjects: bfloat16 [2048, 3, 20480], P(('groups', 'batch'), None, 'patch'), parts along dimension 0, may hold values from -6 to 6
- basis_modes: bfloat16 [3, 40960, 128], P(None, ('groups', 'patch')), parts along dimension 1, may hold values from -21 to 21
- laplace_blocks: bfloat16 [320, 4, 64, 64], P('patch'), may hold values from -0.29882812 to 0.29882812
- columns: int32 [320, 4], P('patch'), may hold values from 0 to 319, as said below
Outputs:
- scores: float32 [2048, 128], P(('groups', 'batch')), parts along dimension 0
- new_modes: bfloat16 [3, 40960, 128], P(None, ('groups', 'patch')), parts along dimension 1
- mode_norms: float32 [256], P('groups'), parts along dimension 0
There are 2 independent parts, one for each index of `groups`. A program takes and returns all parts, laid end to end along the dimension named above; an argument that names none is the same for every part. Nothing has to cross between parts.
Inputs may be any that keep to these rules, and one draw needn't show every extreme that they name: columns[i, 0] = i; with 40 blocks a patch, an entry of block row i lies in i's own patch, except that in the last 4 block rows of a patch an entry may also lie among the first 4 blocks of the next patch; entries of a row may repeat.
All inputs are finite; a program needn't handle non-finite values.
Results may differ from a plain program's by a relative error of at most 0.0034.
Values may be sent and summed in bfloat16 or wider, within the bound.
A program may use at most 192 MiB of HBM per device.

v0:
```python
import math

import jax
import jax.numpy as jnp
from jax import lax
from jax.sharding import PartitionSpec as P


def shifted(value, axis, steps):
    count = lax.axis_size(axis)
    initial, last = (max(0, -steps), min(count, count - steps))
    return lax.ppermute(value, axis, [(source, source + steps) for source in range(initial, last)])


def return_partials(moved, col_terms, local_cols, block_count, reach):
    moved_sum = jax.ops.segment_sum(moved, local_cols, num_segments=block_count + reach)
    col_sum = jax.ops.segment_sum(col_terms, local_cols, num_segments=block_count + reach)
    back_moved, back_cols = (
        shifted(moved_sum[block_count:].astype(jnp.bfloat16), "patch", 1).astype(jnp.float32),
        shifted(col_sum[block_count:].astype(jnp.bfloat16), "patch", 1).astype(jnp.float32),
    )
    total_moved = moved_sum[:block_count].at[:reach].add(back_moved)
    total_cols = col_sum[:block_count].at[:reach].add(back_cols)
    return (total_moved, total_cols)


def body(subjects, basis_modes, laplace_blocks, columns):
    subject_count = subjects.shape[0]
    vert_count = subjects.shape[2]
    mode_count = basis_modes.shape[2]
    per_row = columns.shape[1]
    block_count = vert_count // 64
    coord_count = 3 * vert_count * lax.axis_size("patch")
    scale_inv = 1.0 / math.sqrt(coord_count)
    x_flat = subjects.reshape(subject_count, 3 * vert_count)
    w_flat = basis_modes.reshape(3 * vert_count, mode_count)
    partial_value = jnp.dot(x_flat, w_flat, preferred_element_type=jnp.float32)
    scores = lax.psum(partial_value, "patch") * scale_inv
    score_low = scores.astype(jnp.bfloat16)
    recon = lax.dot_general(
        score_low, w_flat, (((1,), (1,)), ((), ())), preferred_element_type=jnp.float32
    )
    residual = (x_flat.astype(jnp.float32) - recon * scale_inv).astype(jnp.bfloat16)
    patch_id = lax.axis_index("patch")
    grid = basis_modes.reshape(3, block_count, 64, mode_count)
    local_cols = (columns - patch_id * block_count).reshape(-1)
    flat_blocks = laplace_blocks.reshape(block_count * per_row, 64, 64)
    next_part = shifted(basis_modes, "patch", -1)
    next_grid = next_part.reshape(3, block_count, 64, mode_count)
    joined = jnp.concatenate([grid, next_grid], axis=1)
    picked = jnp.take(joined, local_cols, axis=1)
    forward = jnp.einsum("nij,cnjk->cnik", flat_blocks, picked, preferred_element_type=jnp.float32)
    forward = forward.reshape(3, block_count, per_row, 64, mode_count).sum(axis=2)
    blocks_f = laplace_blocks.astype(jnp.float32)
    row_sums = blocks_f.sum(axis=(1, 3))
    col_terms = blocks_f.sum(axis=2).reshape(block_count * per_row, 64)
    moved = jnp.einsum("bnij,cbik->bncjk", laplace_blocks, grid, preferred_element_type=jnp.float32)
    moved = moved.reshape(block_count * per_row, 3, 64, mode_count)
    total_moved, total_cols = return_partials(
        moved, col_terms, local_cols, block_count, block_count
    )
    degree = row_sums + total_cols
    smooth = (
        degree[None, :, :, None] * grid.astype(jnp.float32)
        - forward
        - total_moved.transpose(1, 0, 2, 3)
    )
    smooth = smooth.reshape(3 * vert_count, mode_count)
    all_subjects = subject_count * lax.axis_size("batch")
    hebb = lax.dot_general(
        residual, score_low, (((0,), (0,)), ((), ())), preferred_element_type=jnp.float32
    )
    hebb = lax.psum(hebb, "batch")
    updated = w_flat.astype(jnp.float32) + 4.0 / all_subjects * hebb - 0.2 * smooth
    squares = lax.psum(jnp.sum(updated * updated, axis=0), "patch")
    norms = jnp.sqrt(squares / coord_count + 1e-06)
    new_modes = (updated / norms).astype(jnp.bfloat16).reshape(3, vert_count, mode_count)
    return (scores, new_modes, norms)


def solution(mesh):
    placed = (
        P(("groups", "batch"), None, "patch"),
        P(None, ("groups", "patch"), None),
        P("patch", None, None, None),
        P("patch", None),
    )
    return jax.shard_map(
        body,
        mesh=mesh,
        in_specs=placed,
        out_specs=(P(("groups", "batch"), None), P(None, ("groups", "patch"), None), P("groups")),
        check_vma=False,
    )
```

profile of v0, /device:TPU:0, one launch (start us, length us, event | category | flops | bytes accessed | tf_op | source)
XLA Modules:
  0.0 304.0 jit_solution(7332229887014329966)
XLA Ops:
  7.2 0.0 all-reduce.3.cloned.1.call-start
  7.2 6.7 %convolution_bitcast_fusion.1 = f32[512,128]{1,0:T(8,128)} fusion(bf16[512,3,2560]{2,0,1:T(8,128)(2,1)} %param.12, bf16[3,2560,128]{2,1,0:T(8,128)(2,1)} %param.13), kind=kOutput, calls=%fused_computation.25 | convolution fusion | flops 1006632960 | bytes 10092544 | tf_op jit(solution)/shard_map/dot_general | solution.py:37
  13.9 0.0 all-reduce.5.cloned.1.call-start
  14.0 10.7 %copy.15 = bf16[512,3,2560]{0,2,1:T(8,128)(2,1)} copy(bf16[512,3,2560]{2,0,1:T(8,128)(2,1)} %param.12) | data formatting | bytes 15728640 | tf_op args[0]
  24.7 11.0 %bitcast_convert_fusion = f32[512,7680]{0,1:T(8,128)} fusion(bf16[512,3,2560]{0,2,1:T(8,128)(2,1)} %copy.15), kind=kLoop, calls=%fused_computation.5 | loop fusion | flops 3932160 | bytes 23592960 | tf_op jit(solution)/shard_map/convert_element_type | solution.py:43
  35.7 15.8 %copy.16 = f32[512,7680]{1,0:T(8,128)} copy(f32[512,7680]{0,1:T(8,128)} %bitcast_convert_fusion) | data formatting | bytes 31457280 | tf_op jit(solution)/shard_map/convert_element_type | solution.py:43
  51.5 36.4 %all-reduce.3.cloned.1.call-done = f32[512,128]{1,0:T(8,128)} async-done(((f32[512,128]{1,0:T(8,128)}), f32[512,128]{1,0:T(8,128)}) %all-reduce.3.cloned.1.call-update) | async-done | bytes 262160 | tf_op jit(solution)/shard_map/psum | solution.py:38
  87.8 1.0 broadcast_multiply_fusion
  88.8 11.7 %fusion.9 = f32[7680,128]{1,0:T(8,128)} fusion(f32[512,7680]{1,0:T(8,128)} %copy.16, bf16[7680,128]{1,0:T(8,128)(2,1)S(1)} %bitcast.50, f32[512,128]{1,0:T(8,128)S(1)} %broadcast_multiply_fusion), kind=kOutput, calls=%fused_computation.23 | convolution fusion | flops 2025193472 | bytes 21889024 | tf_op jit(solution)/shard_map/dot_general | solution.py:70
  100.6 1.5 collective-permute-start.1
  102.1 0.1 copy.17
  102.2 0.1 reshape.157
  102.3 10.0 %convolution_bitcast_fusion = f32[40,4,3,64,128]{4,3,1,2,0:T(8,128)} fusion(bf16[40,4,64,64]{3,2,1,0:T(8,128)(2,1)} %param.14, bf16[3,40,64,128,1]{3,2,1,0,4:T(8,128)(2,1)S(1)} %bitcast.51), kind=kOutput, calls=%fused_computation.4 | convolution fusion | flops 503316480 | bytes 19005440 | tf_op jit(solution)/shard_map/bnij,cbik->bncjk/dot_general | solution.py:57
  112.3 14.9 %copy.22 = f32[40,4,3,64,128]{4,3,2,1,0:T(8,128)} copy(f32[40,4,3,64,128]{4,3,1,2,0:T(8,128)} %convolution_bitcast_fusion) | data formatting | bytes 31457280 | tf_op jit(solution)/shard_map/bnij,cbik->bncjk/transpose | solution.py:57
  127.2 4.1 %broadcast_in_dim.21 = f32[80,3,64,128]{3,2,1,0:T(8,128)} broadcast(f32[]{:T(128)} %constant.97.clone.1), dimensions={} | broadcast | bytes 7864324 | tf_op jit(solution)/shard_map/broadcast_in_dim | solution.py:16
  131.3 40.0 %scatter_fusion = f32[80,3,64,128]{3,2,1,0:T(8,128)} fusion(f32[80,3,64,128]{3,2,1,0:T(8,128)} %broadcast_in_dim.21, s32[160]{0:T(256)S(1)} %reshape.157, f32[160,3,64,128]{3,2,1,0:T(8,128)} %bitcast.55), kind=kCustom, calls=%fused_computation.2 | custom fusion | flops 3932160 | bytes 47186560 | tf_op jit(solution)/shard_map/scatter-add | solution.py:16
  171.3 4.0 %slice.74 = bf16[40,3,64,128]{3,2,1,0:T(8,128)(2,1)} slice(f32[80,3,64,128]{3,2,1,0:T(8,128)} %scatter_fusion), slice={[40:80], [0:3], [0:64], [0:128]} | slice | bytes 3932160 | tf_op jit(solution)/shard_map/slice | solution.py:19
  175.3 5.4 %collective-permute-start.2 = (bf16[40,3,64,128]{3,2,1,0:T(8,128)(2,1)}, bf16[40,3,64,128]{3,2,1,0:T(8,128)(2,1)}, u32[]{:S(2)}, u32[]{:S(2)}) collective-permute-start(bf16[40,3,64,128]{3,2,1,0:T(8,128)(2,1)} %slice.74), channel_id=1, source_target_pairs={{0,2},{2,4},{4,6},{6,8},{8,10},{10,12},{12,14},{1,3},{3,5},{5,7},{... | collective-permute-start | bytes 5898248 | tf_op jit(solution)/shard_map/ppermute | solution.py:12
  180.7 0.9 convert_reduce_fusion
  181.6 1.1 scatter_custom_fusion
  182.8 2.6 collective-permute-start
  185.4 0.1 broadcast_in_dim_reshape.4
  185.5 36.1 %collective-permute-done = bf16[40,64]{1,0:T(8,128)(2,1)S(1)} collective-permute-done((bf16[40,64]{1,0:T(8,128)(2,1)S(1)}, bf16[40,64]{1,0:T(8,128)(2,1)S(1)}, u32[]{:S(2)}, u32[]{:S(2)}) %collective-permute-start) | collective-permute-done | bytes 5152 | tf_op jit(solution)/shard_map/ppermute | solution.py:12
  221.6 3.8 %pad_maximum_fusion = bf16[3,80,64,128]{3,2,1,0:T(8,128)(2,1)} fusion(bf16[3,40,64,128]{3,2,1,0:T(8,128)(2,1)} %bitcast.5, bf16[3,40,64,128]{3,2,1,0:T(8,128)(2,1)S(1)} %bitcast.52), kind=kLoop, calls=%fused_computation.17 | loop fusion | flops 1966080 | bytes 7864320 | tf_op jit(solution)/shard_map/concatenate | solution.py:50
  225.4 11.1 %gather_fusion = bf16[160,3,64,128]{3,2,1,0:T(8,128)(2,1)} fusion(bf16[3,80,64,128]{3,2,1,0:T(8,128)(2,1)} %pad_maximum_fusion, s32[1024]{0:T(1024)S(1)} %pad_clamp_fusion), kind=kCustom, calls=%fused_computation | custom fusion | bytes 15729280 | tf_op jit(solution)/shard_map/jit(_take)/gather | solution.py:51
  236.4 11.8 %fusion = f32[160,3,128,64]{2,3,1,0:T(8,128)} fusion(bf16[160,64,64,1]{2,1,3,0:T(8,128)(2,1)} %bitcast.56, bf16[160,3,64,128]{3,2,1,0:T(8,128)(2,1)} %gather_fusion, pred[160]{0:T(512)(128)(4,1)S(1)} %compare_and_fusion), kind=kOutput, calls=%fused_computation.6 | convolution fusion | flops 507248640 | bytes 24903840 | tf_op jit(solution)/shard_map/nij,cnjk->cnik/dot_general | solution.py:52
  248.3 9.8 %reduce_sum.38 = f32[3,40,64,128]{3,2,0,1:T(8,128)} reduce(f32[3,40,4,64,128]{4,3,0,2,1:T(8,128)} %bitcast.54, f32[]{:T(128)} %constant.97.clone.1), dimensions={2}, to_apply=%region_5.6 | reduce | flops 2949120 | bytes 19660804 | tf_op jit(solution)/shard_map/reduce_sum | solution.py:53
  258.1 4.6 %fusion.6 = f32[3,40,64,128]{3,2,0,1:T(8,128)S(1)} fusion(f32[80,3,64,128]{3,2,1,0:T(8,128)} %scatter_fusion, bf16[40,3,64,128]{3,2,1,0:T(8,128)(2,1)} %collective-permute-done.2, f32[3,40,64,128]{3,2,0,1:T(8,128)} %reduce_sum.38, bf16[3,40,64,128]{3,2,1,0:T(8,128)(2,1)S(1)} %bitcast.53, f32[40,64]{1,0:T(8,128)S(1)} %fusion.13), kind=kLoop, calls=%fused_computation.16 | loop fusion | flops 6881280 | bytes 15738880 | tf_op jit(solution)/shard_map/mul | solution.py:74
  262.7 2.2 copy.23
  264.9 4.3 %multiply_reduce_fusion = f32[128]{0:T(128)S(1)} fusion(f32[3,40,64,128]{3,2,1,0:T(8,128)} %copy.23, f32[7680,128]{1,0:T(8,128)} %all-reduce.5.cloned.1.call-done, bf16[3,2560,128]{2,1,0:T(8,128)(2,1)S(1)} %copy-done), kind=kLoop, calls=%fused_computation.21 | loop fusion | flops 5898112 | bytes 9830912 | tf_op jit(solution)/shard_map/reduce_sum | solution.py:75
  269.2 22.5 %psum.23 = f32[128]{0:T(128)S(1)} all-reduce(f32[128]{0:T(128)S(1)} %multiply_reduce_fusion), channel_id=1, replica_groups=mesh['groups'=2,'patch'=8,'batch'=2] {'patch'}, use_global_device_ids=true, to_apply=%region_8.9 | all-reduce | flops 128 | bytes 1024 | tf_op jit(solution)/shard_map/psum | solution.py:75
  291.8 5.4 %divide_convert_fusion = bf16[7680,128]{1,0:T(8,128)(2,1)} fusion(f32[128]{0:T(128)S(1)} %add_sqrt_fusion, f32[3,40,64,128]{3,2,1,0:T(8,128)} %copy.23, f32[7680,128]{1,0:T(8,128)} %all-reduce.5.cloned.1.call-done, bf16[3,2560,128]{2,1,0:T(8,128)(2,1)S(1)} %copy-done), kind=kLoop, calls=%fused_computation.20 | loop fusion | flops 5898240 | bytes 11796992 | tf_op jit(solution)/shard_map/convert_element_type | solution.py:77
  (22 shorter events, 0.1 us)
Async XLA Ops:
  7.2 80.6 %all-reduce.3.cloned.1.call-start = ((), (), s32[]{:S(2)}) async-start(), calls=%async_computation | async-start | bytes 524288 | tf_op jit(solution)/shard_map/psum | solution.py:38
  13.9 251.0 %all-reduce.5.cloned.1.call-start = ((), (), s32[]{:S(2)}) async-start(), calls=%async_computation.1 | async-start | bytes 7864320 | tf_op jit(solution)/shard_map/psum | solution.py:73
  35.7 53.1 %copy-start = (bf16[3,2560,128]{2,1,0:T(8,128)(2,1)S(1)}, bf16[3,2560,128]{2,1,0:T(8,128)(2,1)}, u32[]{:S(2)}) copy-start(bf16[3,2560,128]{2,1,0:T(8,128)(2,1)} %param.13) | copy-start | bytes 5898244
  88.8 11.8 %copy-start.2 = (f32[512,128]{1,0:T(8,128)}, f32[512,128]{1,0:T(8,128)S(1)}, u32[]{:S(2)}) copy-start(f32[512,128]{1,0:T(8,128)S(1)} %broadcast_multiply_fusion) | copy-start | bytes 786436
  100.6 1.5 copy-start.3
  100.6 121.0 %collective-permute-start.1 = (bf16[3,2560,128]{2,1,0:T(8,128)(2,1)S(1)}, bf16[3,2560,128]{2,1,0:T(8,128)(2,1)}, u32[]{:S(2)}, u32[]{:S(2)}) collective-permute-start(bf16[3,2560,128]{2,1,0:T(8,128)(2,1)S(1)} %copy-done), channel_id=1, source_target_pairs={{2,0},{4,2},{6,4},{8,6},{10,8},{12,10},{14,12},{3,1},{5,3},{7,5},{... | collective-permute-start | bytes 5898248 | tf_op jit(solution)/shard_map/ppermute | solution.py:12
  171.3 9.4 %copy-start.1 = (bf16[40,4,64,64]{3,2,1,0:T(8,128)(2,1)S(1)}, bf16[40,4,64,64]{3,2,1,0:T(8,128)(2,1)}, u32[]{:S(2)}) copy-start(bf16[40,4,64,64]{3,2,1,0:T(8,128)(2,1)} %param.14) | copy-start | bytes 3932164
  175.3 82.8 %collective-permute-start.2 = (bf16[40,3,64,128]{3,2,1,0:T(8,128)(2,1)}, bf16[40,3,64,128]{3,2,1,0:T(8,128)(2,1)}, u32[]{:S(2)}, u32[]{:S(2)}) collective-permute-start(bf16[40,3,64,128]{3,2,1,0:T(8,128)(2,1)} %slice.74), channel_id=1, source_target_pairs={{0,2},{2,4},{4,6},{6,8},{8,10},{10,12},{12,14},{1,3},{3,5},{5,7},{... | collective-permute-start | bytes 5898248 | tf_op jit(solution)/shard_map/ppermute | solution.py:12
  182.8 38.8 %collective-permute-start = (bf16[40,64]{1,0:T(8,128)(2,1)S(1)}, bf16[40,64]{1,0:T(8,128)(2,1)S(1)}, u32[]{:S(2)}, u32[]{:S(2)}) collective-permute-start(bf16[40,64]{1,0:T(8,128)(2,1)S(1)} %slice.75), channel_id=1, source_target_pairs={{0,2},{2,4},{4,6},{6,8},{8,10},{10,12},{12,14},{1,3},{3,5},{5,7},{... | collective-permute-start | bytes 15368 | tf_op jit(solution)/shard_map/ppermute | solution.py:12
  291.8 5.4 %copy-start.4 = (f32[128]{0:T(128)}, f32[128]{0:T(128)S(1)}, u32[]{:S(2)}) copy-start(f32[128]{0:T(128)S(1)} %add_sqrt_fusion) | copy-start | bytes 1540
Sparse Core Ops, SparseCore 0:
  14.0 73.7 all-reduce.2
  100.7 24.1 all-reduce.4
where the time goes:
time: 305 us; the launch traced here: 304 us
  other arithmetic  82 us (27%)
  waiting for transfers between devices  72.5 us (24%)
  local copies, waits for them, and re-layouts  63 us (21%)
  matrix products  40.2 us (13%)
  blocking collectives  22.5 us (7%)
  between operations  14.2 us (5%)
  starting transfers between devices  9.6 us (3%)
    scatter-add x1, other arithmetic, return_partials(): jax.ops.segment_sum(moved, local_cols, num_segments=block_count + reach)  40 us
    psum x1, waiting for transfers between devices, body(): scores = lax.psum(partial_value, 'patch') * scale_inv  36.4 us
    ppermute x3, waiting for transfers between devices, shifted(): lax.ppermute(value, axis, [(source, source + steps) for source in range(i...  36.1 us
    psum x1, blocking collectives, body(): squares = lax.psum(jnp.sum(updated * updated, axis=0), 'patch')  22.5 us
    convert_element_type x1, local copies, waits for them, and re-layouts, body(): x_flat.astype(jnp.float32) - recon * scale_inv  15.8 us
    transpose x1, local copies, waits for them, and re-layouts, body(): jnp.einsum('bnij,cbik->bncjk', laplace_blocks, grid, preferred_element_ty...  14.9 us
    dot_general x1, matrix products, body(): jnp.einsum('nij,cnjk->cnik', flat_blocks, picked, preferred_element_type=...  11.8 us
    dot_general x1, matrix products, body(): lax.dot_general(residual, score_low, (((0,), (0,)), ((), ())), preferred_...  11.7 us
  transfers between devices with their start and end apart: 5, of which 2 were waited for; matrix products, arithmetic and copies ran while one was open for 51% of the time, Pallas kernels for 0%

commit v1 on v0

v1 whole, which is shorter than its diff:
```python
import functools
import math

import jax
import jax.numpy as jnp
from jax import lax
from jax.experimental import pallas as pl
from jax.experimental.pallas import tpu as pltpu
from jax.sharding import PartitionSpec as P

GHOST = 4
MESH = pl.DeviceIdType.MESH
VMEM = pl.BlockSpec(memory_space=pltpu.VMEM)
SMEM = pl.BlockSpec(memory_space=pltpu.SMEM)
LIMIT = 60 * 1024 * 1024


def shifted(value, axis, steps):
    count = lax.axis_size(axis)
    initial, last = (max(0, -steps), min(count, count - steps))
    return lax.ppermute(value, axis, [(source, source + steps) for source in range(initial, last)])


def greet(n, axis):
    me = lax.axis_index(axis)
    barrier = pltpu.get_barrier_semaphore()
    for step in range(1, n):
        pl.semaphore_signal(
            barrier, inc=1, device_id={axis: lax.rem(me + step, n)}, device_id_type=MESH
        )
    pl.semaphore_wait(barrier, n - 1)
    return me


def sum_kernel(n, scale, part_ref, out_ref, low_ref, land, full, send_a, recv_a, send_b, recv_b):
    me = greet(n, "patch")
    rows = part_ref.shape[0] // n
    copies = []
    for step in range(1, n):
        to = lax.rem(me + step, n)
        copy = pltpu.make_async_remote_copy(
            src_ref=part_ref.at[pl.ds(pl.multiple_of(to * rows, rows), rows)],
            dst_ref=land.at[step],
            send_sem=send_a.at[step],
            recv_sem=recv_a.at[step],
            device_id={"patch": to},
            device_id_type=MESH,
        )
        copy.start()
        copies.append(copy)
    own = pl.ds(pl.multiple_of(me * rows, rows), rows)
    total = part_ref[own, :]
    for step, copy in enumerate(copies, 1):
        copy.wait()
        total = total + land[step]
    full[own, :] = total * scale
    copies = []
    for step in range(1, n):
        to = lax.rem(me + step, n)
        copy = pltpu.make_async_remote_copy(
            src_ref=full.at[own],
            dst_ref=full.at[own],
            send_sem=send_b.at[step],
            recv_sem=recv_b.at[step],
            device_id={"patch": to},
            device_id_type=MESH,
        )
        copy.start()
        copies.append(copy)
    for copy in copies:
        copy.wait()
    out_ref[...] = full[...]
    low_ref[...] = full[...].astype(jnp.bfloat16)


def reduce_scores(partial_value, scale):
    n = lax.axis_size("patch")
    rows, width = partial_value.shape
    return pl.pallas_call(
        functools.partial(sum_kernel, n, scale),
        out_shape=(
            jax.ShapeDtypeStruct((rows, width), jnp.float32),
            jax.ShapeDtypeStruct((rows, width), jnp.bfloat16),
        ),
        in_specs=[VMEM],
        out_specs=(VMEM, VMEM),
        scratch_shapes=[
            pltpu.VMEM((n, rows // n, width), jnp.float32),
            pltpu.VMEM((rows, width), jnp.float32),
        ]
        + [pltpu.SemaphoreType.DMA((n,))] * 4,
        compiler_params=pltpu.CompilerParams(collective_id=0, has_side_effects=True),
        name="reduce_scores",
    )(partial_value)


def smooth_kernel(cols, back_cols, blocks, back_blocks, modes, after, before, out, wide, acc):
    count, per_row, side, _ = blocks.shape
    coords, verts, width = modes.shape
    reach = after.shape[1]
    ones = jnp.ones((wide.shape[0], width), jnp.bfloat16)
    for c in range(coords):
        lanes = slice(c * width, (c + 1) * width)
        wide[:verts, lanes] = modes[c]
        wide[verts : verts + reach, lanes] = after[c]
        wide[verts + reach :, lanes] = before[c]
    wide[:, coords * width :] = ones
    acc[...] = jnp.zeros_like(acc)

    def rows_of(block):
        return pl.ds(pl.multiple_of(block * side, side), side)

    def scatter(joined, block, targets):
        moved = lax.dot_general(
            joined,
            wide[rows_of(block), :],
            (((0,), (0,)), ((), ())),
            preferred_element_type=jnp.float32,
        )
        for slot, target in enumerate(targets):
            acc[rows_of(target), :] += moved[slot * side : (slot + 1) * side]

    def step(i, _):
        joined = jnp.concatenate([blocks[i, slot] for slot in range(per_row)], axis=1)
        targets = [cols[i, slot] for slot in range(per_row)]
        picked = jnp.concatenate([wide[rows_of(t), :] for t in targets], axis=0)
        acc[rows_of(i), :] += jnp.dot(joined, picked, preferred_element_type=jnp.float32)
        scatter(joined, i, targets)
        return 0

    lax.fori_loop(0, count, step, 0)

    def back_step(i, _):
        joined = jnp.concatenate([back_blocks[i, slot] for slot in range(per_row)], axis=1)
        targets = [back_cols[i, slot] for slot in range(per_row)]
        scatter(joined, count + reach // side + i, targets)
        return 0

    lax.fori_loop(0, back_blocks.shape[0], back_step, 0)

    def finish(i, _):
        rows = rows_of(i)
        degree = acc[rows, coords * width :]
        for c in range(coords):
            mode = modes[c, rows, :].astype(jnp.float32)
            out[c, rows, :] = mode - 0.2 * (
                degree * mode - acc[rows, c * width : (c + 1) * width]
            )
        return 0

    lax.fori_loop(0, count, finish, 0)


def smoothed(basis_modes, laplace_blocks, columns):
    count, per_row, side, _ = laplace_blocks.shape
    coords, verts, width = basis_modes.shape
    reach = GHOST * side
    first = lax.axis_index("patch") * count
    after = shifted(basis_modes[:, :reach], "patch", -1)
    before = shifted(basis_modes[:, verts - reach :], "patch", 1)
    back_blocks = shifted(laplace_blocks[count - GHOST :], "patch", 1)
    back_cols = shifted(columns[count - GHOST :], "patch", 1)
    total = count + 2 * GHOST
    cols = columns - first
    back = back_cols - first
    back = jnp.where((back >= 0) & (back < GHOST), back, total - 1)
    return pl.pallas_call(
        smooth_kernel,
        out_shape=jax.ShapeDtypeStruct((coords, verts, width), jnp.float32),
        in_specs=[SMEM, SMEM] + [VMEM] * 5,
        out_specs=VMEM,
        scratch_shapes=[
            pltpu.VMEM((total * side, (coords + 1) * width), jnp.bfloat16),
            pltpu.VMEM((total * side, (coords + 1) * width), jnp.float32),
        ],
        compiler_params=pltpu.CompilerParams(vmem_limit_bytes=LIMIT),
        name="smooth",
    )(cols, back, laplace_blocks, back_blocks, basis_modes, after, before)


def hebb_kernel(scale, x_ref, low_ref, turned_ref, mode_ref, out_ref):
    recon = lax.dot_general(
        low_ref[...], mode_ref[0], (((1,), (1,)), ((), ())), preferred_element_type=jnp.float32
    )
    residual = (x_ref[0].astype(jnp.float32) - recon * scale).astype(jnp.bfloat16)
    hebb = jnp.dot(turned_ref[...], residual, preferred_element_type=jnp.float32)
    out_ref[0] = hebb.T.astype(jnp.bfloat16)


def hebbian(planes, low, basis_modes, scale):
    coords, subjects, verts = planes.shape
    width = basis_modes.shape[2]
    tile = math.gcd(verts, 512)
    return pl.pallas_call(
        functools.partial(hebb_kernel, scale),
        out_shape=jax.ShapeDtypeStruct((coords, verts, width), jnp.bfloat16),
        grid=(coords, verts // tile),
        in_specs=[
            pl.BlockSpec((1, subjects, tile), lambda c, v: (c, 0, v)),
            pl.BlockSpec((subjects, width), lambda c, v: (0, 0)),
            pl.BlockSpec((width, subjects), lambda c, v: (0, 0)),
            pl.BlockSpec((1, tile, width), lambda c, v: (c, v, 0)),
        ],
        out_specs=pl.BlockSpec((1, tile, width), lambda c, v: (c, v, 0)),
        compiler_params=pltpu.CompilerParams(vmem_limit_bytes=LIMIT),
        name="hebb",
    )(planes, low, low.T, basis_modes)


def finish_kernel(n, rate, coord_count, base, mine, other, out, norms, updated, slots, send, recv):
    rows = base.shape[0]
    width = base.shape[1]
    piece = math.gcd(rows, 256)

    def update(i, sums):
        here = pl.ds(pl.multiple_of(i * piece, piece), piece)
        both = mine[here, :].astype(jnp.float32) + other[here, :].astype(jnp.float32)
        value = base[here, :] + rate * both
        updated[here, :] = value
        return sums + jnp.sum((value * value).reshape(piece // 8, 8, width), axis=0)

    sums = lax.fori_loop(0, rows // piece, update, jnp.zeros((8, width), jnp.float32))
    me = greet(n, "patch")
    slots[me] = sums
    copies = []
    for step in range(1, n):
        copy = pltpu.make_async_remote_copy(
            src_ref=slots.at[me],
            dst_ref=slots.at[me],
            send_sem=send.at[step],
            recv_sem=recv.at[step],
            device_id={"patch": lax.rem(me + step, n)},
            device_id_type=MESH,
        )
        copy.start()
        copies.append(copy)
    for copy in copies:
        copy.wait()
    squares = jnp.sum(jnp.sum(slots[...], axis=0), axis=0, keepdims=True)
    norm = jnp.sqrt(squares / coord_count + 1e-06)
    norms[...] = norm

    def divide(i, _):
        here = pl.ds(pl.multiple_of(i * piece, piece), piece)
        out[here, :] = (updated[here, :] / norm).astype(jnp.bfloat16)
        return 0

    lax.fori_loop(0, rows // piece, divide, 0)


def finished(base, mine, other, rate, coord_count):
    n = lax.axis_size("patch")
    rows, width = base.shape
    return pl.pallas_call(
        functools.partial(finish_kernel, n, rate, coord_count),
        out_shape=(
            jax.ShapeDtypeStruct((rows, width), jnp.bfloat16),
            jax.ShapeDtypeStruct((1, width), jnp.float32),
        ),
        in_specs=[VMEM] * 3,
        out_specs=(VMEM, VMEM),
        scratch_shapes=[
            pltpu.VMEM((rows, width), jnp.float32),
            pltpu.VMEM((n, 8, width), jnp.float32),
            pltpu.SemaphoreType.DMA((n,)),
            pltpu.SemaphoreType.DMA((n,)),
        ],
        compiler_params=pltpu.CompilerParams(
            collective_id=1, has_side_effects=True, vmem_limit_bytes=LIMIT
        ),
        name="finish",
    )(base, mine, other)


def body(subjects, basis_modes, laplace_blocks, columns):
    subject_count, coords, vert_count = subjects.shape
    mode_count = basis_modes.shape[2]
    batch = lax.axis_size("batch")
    coord_count = coords * vert_count * lax.axis_size("patch")
    scale_inv = 1.0 / math.sqrt(coord_count)
    planes = subjects.transpose(1, 0, 2)
    partial_value = lax.dot_general(
        subjects, basis_modes, (((1, 2), (0, 1)), ((), ())), preferred_element_type=jnp.float32
    )
    scores, low = reduce_scores(partial_value, scale_inv)
    base = smoothed(basis_modes, laplace_blocks, columns)
    hebb = hebbian(planes, low, basis_modes, scale_inv)
    other = lax.ppermute(hebb, "batch", [(i, (i + 1) % batch) for i in range(batch)])
    flat = (coords * vert_count, mode_count)
    rate = 4.0 / (subject_count * batch)
    new_modes, norms = finished(
        base.reshape(flat), hebb.reshape(flat), other.reshape(flat), rate, coord_count
    )
    return (scores, new_modes.reshape(coords, vert_count, mode_count), norms.reshape(mode_count))


def solution(mesh):
    placed = (
        P(("groups", "batch"), None, "patch"),
        P(None, ("groups", "patch"), None),
        P("patch", None, None, None),
        P("patch", None),
    )
    return jax.shard_map(
        body,
        mesh=mesh,
        in_specs=placed,
        out_specs=(P(("groups", "batch"), None), P(None, ("groups", "patch"), None), P("groups")),
        check_vma=False,
    )
```

time: 305 us -> 108 us (0.35)
  other arithmetic: 82 us -> 1.2 us
  Pallas kernels: 0 us -> 70 us
  waiting for transfers between devices: 72.5 us -> 7.4 us
  local copies, waits for them, and re-layouts: 63 us -> 10.6 us
  matrix products: 40.2 us -> 6.68 us
  blocking collectives: 22.5 us -> 0 us
  between operations: 14.2 us -> 0.71 us
    pallas_call x0 -> x4, Pallas kernels: none -> 70 us  [the longest x1 20.3 us: smoothed(): pl.pallas_call(smooth_kernel, out_shape=jax.ShapeDtypeStruct((coords, ver...]
    scatter-add x2 -> x0, other arithmetic: 41.1 us -> none  [the longest x1 40 us: return_partials(): jax.ops.segment_sum(moved, local_cols, num_segments=block_count + reach)]
    psum x2 -> x0, waiting for transfers between devices: 36.4 us -> none  [the longest x1 36.4 us: body(): scores = lax.psum(partial_value, 'patch') * scale_inv]
    dot_general x4 -> x1, matrix products: 40.2 us -> 6.68 us  [body(): lax.dot_general(subjects, basis_modes, (((1, 2), (0, 1)), ((), ())), pref...]
    ppermute x3 -> x4, waiting for transfers between devices: 36.1 us -> 7.4 us  [shifted(): lax.ppermute(value, axis, [(source, source + steps) for source in range(i...]
    psum x1 -> x0, blocking collectives: 22.5 us -> none  [body(): squares = lax.psum(jnp.sum(updated * updated, axis=0), 'patch')]
    convert_element_type x2 -> x0, other arithmetic: 16.4 us -> none  [the longest x1 11 us: body(): x_flat.astype(jnp.float32) - recon * scale_inv]
    convert_element_type x1 -> x0, local copies, waits for them, and re-layouts: 15.8 us -> none  [body(): x_flat.astype(jnp.float32) - recon * scale_inv]
  transfers between devices with their start and end apart: 5 -> 5, of which waited for: 2 -> 1; matrix products, arithmetic and copies ran while one was open for 51% -> 3% of each run, Pallas kernels for 0% -> 19%
where the time goes in v1:
time: 108 us
  Pallas kernels  70 us (65%)
  starting transfers between devices  11.2 us (10%)
  local copies, waits for them, and re-layouts  10.6 us (10%)
  waiting for transfers between devices  7.4 us (7%)
  matrix products  6.68 us (6%)
  other arithmetic  1.2 us (1%)
    pallas_call x1, Pallas kernels, smoothed(): pl.pallas_call(smooth_kernel, out_shape=jax.ShapeDtypeStruct((coords, ver...  20.3 us
    pallas_call x1, Pallas kernels, reduce_scores(): pl.pallas_call(functools.partial(sum_kernel, n, scale), out_shape=(jax.Sh...  20 us
    pallas_call x1, Pallas kernels, finished(): pl.pallas_call(functools.partial(finish_kernel, n, rate, coord_count), ou...  15.4 us
    pallas_call x1, Pallas kernels, hebbian(): pl.pallas_call(functools.partial(hebb_kernel, scale), out_shape=jax.Shape...  14.3 us
    ppermute x4, starting transfers between devices, shifted(): lax.ppermute(value, axis, [(source, source + steps) for source in range(i...  11.2 us
    ppermute x4, waiting for transfers between devices, shifted(): lax.ppermute(value, axis, [(source, source + steps) for source in range(i...  7.4 us
    unnamed x18, local copies, waits for them, and re-layouts  6.89 us
    dot_general x1, matrix products, body(): lax.dot_general(subjects, basis_modes, (((1, 2), (0, 1)), ((), ())), pref...  6.68 us
  transfers between devices with their start and end apart: 5, of which 1 were waited for; matrix products, arithmetic and copies ran while one was open for 3% of the time, Pallas kernels for 19%

profile of v1, /device:TPU:0, one launch (start us, length us, event | category | flops | bytes accessed | tf_op | source)
XLA Modules:
  0.0 107.8 jit_solution(2569775040638396509)
XLA Ops:
  0.6 6.7 %convolution_bitcast_fusion.part_ref = f32[512,128]{1,0:T(8,128)} fusion(bf16[512,3,2560]{2,0,1:T(8,128)(2,1)} %param.4, bf16[3,2560,128]{2,1,0:T(8,128)(2,1)} %mode_ref.1), kind=kOutput, calls=%fused_computation | convolution fusion | flops 1006632960 | bytes 10092544 | tf_op jit(solution)/shard_map/dot_general | solution.py:282
  7.3 20.0 %reduce_scores.1 = (f32[512,128]{1,0:T(8,128)}, bf16[512,128]{1,0:T(8,128)(2,1)}) custom-call(f32[512,128]{1,0:T(8,128)} %convolution_bitcast_fusion.part_ref), custom_call_target="tpu_custom_call" | custom-call | tf_op jit(solution)/shard_map/reduce_scores/pallas_call | solution.py:79
  27.3 1.7 %copy.13 = bf16[512,128]{0,1:T(8,128)(2,1)} copy(bf16[512,128]{1,0:T(8,128)(2,1)} %get-tuple-element.8.low_ref) | data formatting | bytes 262144 | tf_op jit(solution)/shard_map/reduce_scores/pallas_call | solution.py:79
  28.9 0.0 copy-start.5
  28.9 14.3 %hebb.1 = bf16[3,2560,128]{2,1,0:T(8,128)(2,1)} custom-call(bf16[3,512,2560]{2,1,0:T(8,128)(2,1)} %bitcast.12, bf16[512,128]{1,0:T(8,128)(2,1)} %get-tuple-element.8.low_ref, bf16[128,512]{1,0:T(8,128)(2,1)} %bitcast.16, bf16[3,2560,128]{2,1,0:T(8,128)(2,1)} %mode_ref.1), custom_call_target="tpu_custom_call" | custom-call | tf_op jit(solution)/shard_map/hebb/pallas_call | solution.py:194
  43.3 0.0 collective-permute-start.4
  43.3 0.0 copy-done.5
  43.3 0.1 copy.10
  43.4 3.3 %collective-permute-start = (s32[4,4]{1,0:T(4,128)S(1)}, s32[4,4]{1,0:T(4,128)S(1)}, u32[]{:S(2)}, u32[]{:S(2)}) collective-permute-start(s32[4,4]{1,0:T(4,128)S(1)} %slice.16), channel_id=1, source_target_pairs={{0,2},{2,4},{4,6},{6,8},{8,10},{10,12},{12,14},{1,3},{3,5},{5,7},{... | collective-permute-start | bytes 200 | tf_op jit(solution)/shard_map/ppermute | solution.py:21
  46.7 1.0 slice.13
  47.7 3.2 %collective-permute-start.1 = (bf16[4,4,64,64]{3,2,1,0:T(8,128)(2,1)S(1)}, bf16[4,4,64,64]{3,2,1,0:T(8,128)(2,1)S(1)}, u32[]{:S(2)}, u32[]{:S(2)}) collective-permute-start(bf16[4,4,64,64]{3,2,1,0:T(8,128)(2,1)S(1)} %slice.13), channel_id=1, source_target_pairs={{0,2},{2,4},{4,6},{6,8},{8,10},{10,12},{12,14},{1,3},{3,5},{5,7},{... | collective-permute-start | bytes 393224 | tf_op jit(solution)/shard_map/ppermute | solution.py:21
  50.9 1.1 fusion
  51.9 3.4 %collective-permute-start.3 = (bf16[3,256,128]{2,1,0:T(8,128)(2,1)S(1)}, bf16[3,256,128]{2,1,0:T(8,128)(2,1)S(1)}, u32[]{:S(2)}, u32[]{:S(2)}) collective-permute-start(bf16[3,256,128]{2,1,0:T(8,128)(2,1)S(1)} %get-tuple-element.11), channel_id=1, source_target_pairs={{0,2},{2,4},{4,6},{6,8},{8,10},{10,12},{12,14},{1,3},{3,5},{5,7},{... | collective-permute-start | bytes 589832 | tf_op jit(solution)/shard_map/ppermute | solution.py:21
  55.3 1.3 %collective-permute-start.2 = (bf16[3,256,128]{2,1,0:T(8,128)(2,1)S(1)}, bf16[3,256,128]{2,1,0:T(8,128)(2,1)S(1)}, u32[]{:S(2)}, u32[]{:S(2)}) collective-permute-start(bf16[3,256,128]{2,1,0:T(8,128)(2,1)S(1)} %get-tuple-element.12), channel_id=1, source_target_pairs={{2,0},{4,2},{6,4},{8,6},{10,8},{12,10},{14,12},{3,1},{5,3},{7,5},{... | collective-permute-start | bytes 589832 | tf_op jit(solution)/shard_map/ppermute | solution.py:21
  56.6 0.6 broadcast_subtract_fusion.cols
  57.2 0.0 collective-permute-done
  57.2 0.6 and_select_fusion.back_cols
  57.8 0.0 collective-permute-done.1.back_blocks
  57.8 7.4 %collective-permute-done.3.before = bf16[3,256,128]{2,1,0:T(8,128)(2,1)S(1)} collective-permute-done((bf16[3,256,128]{2,1,0:T(8,128)(2,1)S(1)}, bf16[3,256,128]{2,1,0:T(8,128)(2,1)S(1)}, u32[]{:S(2)}, u32[]{:S(2)}) %collective-permute-start.3) | collective-permute-done | bytes 196640 | tf_op jit(solution)/shard_map/ppermute | solution.py:21
  65.2 0.0 collective-permute-done.2.after
  65.2 0.0 copy-done.1
  65.2 0.7 copy-done.3
  65.9 0.7 copy-done.4
  66.6 20.3 %smooth.1 = f32[3,2560,128]{2,1,0:T(8,128)} custom-call(s32[40,4]{1,0:T(8,128)} %broadcast_subtract_fusion.cols, s32[4,4]{1,0:T(4,128)} %and_select_fusion.back_cols, bf16[40,4,64,64]{3,2,1,0:T(8,128)(2,1)} %blocks.1, bf16[4,4,64,64]{3,2,1,0:T(8,128)(2,1)} %copy-done.1, bf16[3,2560,128]{2,1,0:T(8,128)(2,1)} %mode_ref.1, bf16[3,256,128]{2,1,0:T(8,128)(2,1)} %copy-done.4, ...), custom_call_target="tpu_custom_call" | custom-call | tf_op jit(solution)/shard_map/smooth/pallas_call | solution.py:167
  86.9 0.0 collective-permute-done.4
  86.9 1.3 %copy-done = bf16[3,2560,128]{2,1,0:T(8,128)(2,1)} copy-done((bf16[3,2560,128]{2,1,0:T(8,128)(2,1)}, bf16[3,2560,128]{2,1,0:T(8,128)(2,1)S(1)}, u32[]{:S(2)}) %copy-start) | copy-done | bytes 1966104
  88.1 15.4 %finish.1 = (bf16[7680,128]{1,0:T(8,128)(2,1)}, f32[1,128]{1,0:T(1,128)}) custom-call(f32[7680,128]{1,0:T(8,128)} %bitcast.11, bf16[7680,128]{1,0:T(8,128)(2,1)} %bitcast.13, bf16[7680,128]{1,0:T(8,128)(2,1)} %bitcast.15), custom_call_target="tpu_custom_call" | custom-call | tf_op jit(solution)/shard_map/finish/pallas_call | solution.py:254
  103.6 0.0 copy-done.2
  103.6 0.7 copy.17
  104.3 2.9 %copy.18 = bf16[3,2560,128]{2,1,0:T(8,128)(2,1)} copy(bf16[3,2560,128]{2,1,0:T(8,128)(2,1)} %bitcast.14) | data formatting | bytes 3932160
  107.2 0.0 copy-done.6
  107.2 0.5 copy.19
  (7 shorter events, 0.0 us)
Async XLA Ops:
  28.9 14.3 %copy-start.5 = (s32[40,4]{0,1:T(4,128)S(1)}, s32[40,4]{0,1:T(4,128)}, u32[]{:S(2)}) copy-start(s32[40,4]{0,1:T(4,128)} %param.7) | copy-start | bytes 1924
  43.3 43.6 %collective-permute-start.4 = (bf16[3,2560,128]{2,1,0:T(8,128)(2,1)}, bf16[3,2560,128]{2,1,0:T(8,128)(2,1)S(1)}, u32[]{:S(2)}, u32[]{:S(2)}) collective-permute-start(bf16[3,2560,128]{2,1,0:T(8,128)(2,1)} %hebb.1), channel_id=1, source_target_pairs={{0,1},{1,0},{2,3},{3,2},{4,5},{5,4},{6,7},{7,6},{8,9},{9,8},{10,11... | collective-permute-start | bytes 5898248 | tf_op jit(solution)/shard_map/ppermute | solution.py:288
  43.4 13.9 %collective-permute-start = (s32[4,4]{1,0:T(4,128)S(1)}, s32[4,4]{1,0:T(4,128)S(1)}, u32[]{:S(2)}, u32[]{:S(2)}) collective-permute-start(s32[4,4]{1,0:T(4,128)S(1)} %slice.16), channel_id=1, source_target_pairs={{0,2},{2,4},{4,6},{6,8},{8,10},{10,12},{12,14},{1,3},{3,5},{5,7},{... | collective-permute-start | bytes 200 | tf_op jit(solution)/shard_map/ppermute | solution.py:21
  47.7 10.2 %collective-permute-start.1 = (bf16[4,4,64,64]{3,2,1,0:T(8,128)(2,1)S(1)}, bf16[4,4,64,64]{3,2,1,0:T(8,128)(2,1)S(1)}, u32[]{:S(2)}, u32[]{:S(2)}) collective-permute-start(bf16[4,4,64,64]{3,2,1,0:T(8,128)(2,1)S(1)} %slice.13), channel_id=1, source_target_pairs={{0,2},{2,4},{4,6},{6,8},{8,10},{10,12},{12,14},{1,3},{3,5},{5,7},{... | collective-permute-start | bytes 393224 | tf_op jit(solution)/shard_map/ppermute | solution.py:21
  51.9 13.3 %collective-permute-start.3 = (bf16[3,256,128]{2,1,0:T(8,128)(2,1)S(1)}, bf16[3,256,128]{2,1,0:T(8,128)(2,1)S(1)}, u32[]{:S(2)}, u32[]{:S(2)}) collective-permute-start(bf16[3,256,128]{2,1,0:T(8,128)(2,1)S(1)} %get-tuple-element.11), channel_id=1, source_target_pairs={{0,2},{2,4},{4,6},{6,8},{8,10},{10,12},{12,14},{1,3},{3,5},{5,7},{... | collective-permute-start | bytes 589832 | tf_op jit(solution)/shard_map/ppermute | solution.py:21
  55.3 9.9 %collective-permute-start.2 = (bf16[3,256,128]{2,1,0:T(8,128)(2,1)S(1)}, bf16[3,256,128]{2,1,0:T(8,128)(2,1)S(1)}, u32[]{:S(2)}, u32[]{:S(2)}) collective-permute-start(bf16[3,256,128]{2,1,0:T(8,128)(2,1)S(1)} %get-tuple-element.12), channel_id=1, source_target_pairs={{2,0},{4,2},{6,4},{8,6},{10,8},{12,10},{14,12},{3,1},{5,3},{7,5},{... | collective-permute-start | bytes 589832 | tf_op jit(solution)/shard_map/ppermute | solution.py:21
  57.8 7.4 %copy-start.1 = (bf16[4,4,64,64]{3,2,1,0:T(8,128)(2,1)}, bf16[4,4,64,64]{3,2,1,0:T(8,128)(2,1)S(1)}, u32[]{:S(2)}) copy-start(bf16[4,4,64,64]{3,2,1,0:T(8,128)(2,1)S(1)} %collective-permute-done.1.back_blocks) | copy-start | bytes 393220
  65.2 0.7 copy-start.3
  65.9 0.7 copy-start.4
  86.9 1.3 %copy-start = (bf16[3,2560,128]{2,1,0:T(8,128)(2,1)}, bf16[3,2560,128]{2,1,0:T(8,128)(2,1)S(1)}, u32[]{:S(2)}) copy-start(bf16[3,2560,128]{2,1,0:T(8,128)(2,1)S(1)} %collective-permute-done.4) | copy-start | bytes 5898244
  88.1 15.4 %copy-start.2 = (f32[512,128]{1,0:T(8,128)S(1)}, f32[512,128]{1,0:T(8,128)}, u32[]{:S(2)}) copy-start(f32[512,128]{1,0:T(8,128)} %get-tuple-element.16) | copy-start | bytes 786436
  104.3 2.9 %copy-start.6 = (f32[1,128]{1,0:T(1,128)S(1)}, f32[1,128]{1,0:T(1,128)}, u32[]{:S(2)}) copy-start(f32[1,128]{1,0:T(1,128)} %get-tuple-element.10) | copy-start | bytes 1540

commit v2 on v1

v2 whole, which is shorter than its diff:
```python
import functools
import math

import jax
import jax.numpy as jnp
from jax import lax
from jax.experimental import pallas as pl
from jax.experimental.pallas import tpu as pltpu
from jax.sharding import PartitionSpec as P

GHOST = 4
MESH = pl.DeviceIdType.MESH
VMEM = pl.BlockSpec(memory_space=pltpu.VMEM)
ANY = pl.BlockSpec(memory_space=pl.ANY)
SMEM = pl.BlockSpec(memory_space=pltpu.SMEM)
LIMIT = 60 * 1024 * 1024


def greet(axes):
    barrier = pltpu.get_barrier_semaphore()
    peers = 0
    for axis in axes:
        n, me = lax.axis_size(axis), lax.axis_index(axis)
        for step in range(1, n):
            pl.semaphore_signal(
                barrier, inc=1, device_id={axis: lax.rem(me + step, n)}, device_id_type=MESH
            )
        peers += n - 1
    pl.semaphore_wait(barrier, peers)


def sum_kernel(
    n, scale, reach, part_ref, modes, blocks, columns, out_ref, low_ref, turned_ref,
    after, before, back_blocks, back_cols, land, full, send_a, recv_a, send_b, recv_b, send_c, recv_c,
):
    greet(("patch",))
    me = lax.axis_index("patch")
    rows = part_ref.shape[0] // n

    def start(source, target, to, send, recv):
        copy = pltpu.make_async_remote_copy(
            src_ref=source,
            dst_ref=target,
            send_sem=send,
            recv_sem=recv,
            device_id={"patch": to},
            device_id_type=MESH,
        )
        copy.start()
        return copy

    copies = []
    for step in range(1, n):
        to = lax.rem(me + step, n)
        source = part_ref.at[pl.ds(pl.multiple_of(to * rows, rows), rows)]
        copies.append(start(source, land.at[step], to, send_a.at[step], recv_a.at[step]))
    following, previous = lax.rem(me + 1, n), lax.rem(me + n - 1, n)
    verts, count = modes.shape[1], blocks.shape[0]
    edges = []
    for index, (source, target, to) in enumerate((
        (blocks.at[pl.ds(count - GHOST, GHOST)], back_blocks, following),
        (columns, back_cols, following),
        (modes.at[:, pl.ds(verts - reach, reach)], before, following),
        (modes.at[:, pl.ds(0, reach)], after, previous),
    )):
        edges.append(start(source, target, to, send_c.at[index], recv_c.at[index]))
    own = pl.ds(pl.multiple_of(me * rows, rows), rows)
    total = part_ref[own, :]
    for step, copy in enumerate(copies, 1):
        copy.wait()
        total = total + land[step]
    full[own, :] = (total * scale).astype(jnp.bfloat16)
    copies = []
    for step in range(1, n):
        to = lax.rem(me + step, n)
        copies.append(start(full.at[own], full.at[own], to, send_b.at[step], recv_b.at[step]))
    for copy in copies:
        copy.wait()
    scores = full[...].astype(jnp.float32)
    out_ref[...] = scores
    low_ref[...] = full[...]
    turned_ref[...] = scores.T.astype(jnp.bfloat16)
    for copy in edges:
        copy.wait()


def reduce_scores(partial_value, basis_modes, laplace_blocks, columns, scale):
    n = lax.axis_size("patch")
    rows, width = partial_value.shape
    coords = basis_modes.shape[0]
    per_row, side = laplace_blocks.shape[1:3]
    reach = GHOST * side
    chunk = pltpu.VMEM((n, rows // n, width), jnp.float32)
    return pl.pallas_call(
        functools.partial(sum_kernel, n, scale, reach),
        out_shape=(
            jax.ShapeDtypeStruct((rows, width), jnp.float32),
            jax.ShapeDtypeStruct((rows, width), jnp.bfloat16),
            jax.ShapeDtypeStruct((width, rows), jnp.bfloat16),
            jax.ShapeDtypeStruct((coords, reach, width), jnp.bfloat16),
            jax.ShapeDtypeStruct((coords, reach, width), jnp.bfloat16),
            jax.ShapeDtypeStruct((GHOST, per_row, side, side), jnp.bfloat16),
            jax.ShapeDtypeStruct(columns.shape, columns.dtype),
        ),
        in_specs=[VMEM, ANY, ANY, VMEM],
        out_specs=(VMEM, VMEM, VMEM, ANY, ANY, ANY, VMEM),
        scratch_shapes=[chunk, pltpu.VMEM((rows, width), jnp.bfloat16)]
        + [pltpu.SemaphoreType.DMA((n,))] * 4
        + [pltpu.SemaphoreType.DMA((4,))] * 2,
        compiler_params=pltpu.CompilerParams(collective_id=0, has_side_effects=True),
        name="reduce_scores",
    )(partial_value, basis_modes, laplace_blocks, columns)


def smooth_kernel(cols, back_cols, blocks, back_blocks, modes, after, before, out, wide, acc):
    count, per_row, side, _ = blocks.shape
    coords, verts, width = modes.shape
    reach = after.shape[1]
    ones = jnp.ones((wide.shape[0], width), jnp.bfloat16)
    for c in range(coords):
        lanes = slice(c * width, (c + 1) * width)
        wide[:verts, lanes] = modes[c]
        wide[verts : verts + reach, lanes] = after[c]
        wide[verts + reach :, lanes] = before[c]
    wide[:, coords * width :] = ones
    acc[...] = jnp.zeros_like(acc)

    def rows_of(block):
        return pl.ds(pl.multiple_of(block * side, side), side)

    def scatter(joined, block, targets):
        moved = lax.dot_general(
            joined,
            wide[rows_of(block), :],
            (((0,), (0,)), ((), ())),
            preferred_element_type=jnp.float32,
        )
        for slot, target in enumerate(targets):
            acc[rows_of(target), :] += moved[slot * side : (slot + 1) * side]

    group = math.gcd(count, 4)

    def step(outer, _):
        for inner in range(group):
            i = outer * group + inner
            joined = jnp.concatenate([blocks[i, slot] for slot in range(per_row)], axis=1)
            targets = [cols[i, slot] for slot in range(per_row)]
            picked = jnp.concatenate([wide[rows_of(t), :] for t in targets], axis=0)
            acc[rows_of(i), :] += jnp.dot(joined, picked, preferred_element_type=jnp.float32)
            scatter(joined, i, targets)
        return 0

    lax.fori_loop(0, count // group, step, 0)

    def back_step(i, _):
        joined = jnp.concatenate([back_blocks[i, slot] for slot in range(per_row)], axis=1)
        targets = [back_cols[i, slot] for slot in range(per_row)]
        scatter(joined, count + reach // side + i, targets)
        return 0

    lax.fori_loop(0, back_blocks.shape[0], back_step, 0)

    def finish(i, _):
        rows = rows_of(i)
        degree = acc[rows, coords * width :]
        for c in range(coords):
            mode = modes[c, rows, :].astype(jnp.float32)
            out[c, rows, :] = mode - 0.2 * (
                degree * mode - acc[rows, c * width : (c + 1) * width]
            )
        return 0

    lax.fori_loop(0, count, finish, 0)


def smoothed(basis_modes, laplace_blocks, columns, after, before, back_blocks, back_cols):
    count, per_row, side, _ = laplace_blocks.shape
    coords, verts, width = basis_modes.shape
    first = lax.axis_index("patch") * count
    total = count + 2 * GHOST
    cols = columns - first
    back = back_cols[count - GHOST :] - first
    back = jnp.where((back >= 0) & (back < GHOST), back, total - 1)
    return pl.pallas_call(
        smooth_kernel,
        out_shape=jax.ShapeDtypeStruct((coords, verts, width), jnp.float32),
        in_specs=[SMEM, SMEM] + [VMEM] * 5,
        out_specs=VMEM,
        scratch_shapes=[
            pltpu.VMEM((total * side, (coords + 1) * width), jnp.bfloat16),
            pltpu.VMEM((total * side, (coords + 1) * width), jnp.float32),
        ],
        compiler_params=pltpu.CompilerParams(vmem_limit_bytes=LIMIT),
        name="smooth",
    )(cols, back, laplace_blocks, back_blocks, basis_modes, after, before)


def update_kernel(
    scale, rate, coord_count, planes, base, modes, low, turned, out, norms,
    held, updated, both, slots, load, send_h, recv_h, send_n, recv_n,
):
    n, me = lax.axis_size("patch"), lax.axis_index("patch")
    pair, half = lax.axis_size("batch"), lax.axis_index("batch")
    tiles, subjects, tile = held.shape
    coords, verts, width = modes.shape
    per = verts // tile
    loads = []
    for i in range(tiles):
        source = planes.at[i // per, :, pl.ds((i % per) * tile, tile)]
        loads.append(pltpu.make_async_copy(source, held.at[i], load.at[i]))
        loads[-1].start()
    loads.append(pltpu.make_async_copy(base, updated, load.at[tiles]))
    loads[-1].start()
    greet(("patch", "batch"))

    copies = []
    for i in range(tiles):
        mode = modes[i // per, (i % per) * tile : (i % per + 1) * tile, :]
        loads[i].wait()
        recon = lax.dot_general(
            low[...], mode, (((1,), (1,)), ((), ())), preferred_element_type=jnp.float32
        )
        residual = (held[i].astype(jnp.float32) - recon * scale).astype(jnp.bfloat16)
        hebb = jnp.dot(turned[...], residual, preferred_element_type=jnp.float32)
        rows = pl.ds(i * tile, tile)
        both[half, rows, :] = hebb.T.astype(jnp.bfloat16)
        for step in range(1, pair):
            copy = pltpu.make_async_remote_copy(
                src_ref=both.at[half, rows],
                dst_ref=both.at[half, rows],
                send_sem=send_h.at[step, i],
                recv_sem=recv_h.at[step, i],
                device_id={"batch": lax.rem(half + step, pair)},
                device_id_type=MESH,
            )
            copy.start()
            copies.append(copy)
    for copy in copies:
        copy.wait()
    loads[tiles].wait()

    piece = math.gcd(coords * verts, 256)

    def update(i, sums):
        here = pl.ds(pl.multiple_of(i * piece, piece), piece)
        hebb = both[0, here, :].astype(jnp.float32)
        for other in range(1, pair):
            hebb = hebb + both[other, here, :].astype(jnp.float32)
        value = updated[here, :] + rate * hebb
        updated[here, :] = value
        return sums + jnp.sum((value * value).reshape(piece // 8, 8, width), axis=0)

    count = coords * verts // piece
    slots[me] = lax.fori_loop(0, count, update, jnp.zeros((8, width), jnp.float32))
    copies = []
    for step in range(1, n):
        copy = pltpu.make_async_remote_copy(
            src_ref=slots.at[me],
            dst_ref=slots.at[me],
            send_sem=send_n.at[step],
            recv_sem=recv_n.at[step],
            device_id={"patch": lax.rem(me + step, n)},
            device_id_type=MESH,
        )
        copy.start()
        copies.append(copy)
    for copy in copies:
        copy.wait()
    squares = jnp.sum(jnp.sum(slots[...], axis=0), axis=0, keepdims=True)
    norm = jnp.sqrt(squares / coord_count + 1e-06)
    norms[...] = norm
    inverse = 1.0 / norm

    def divide(i, _):
        here = pl.ds(pl.multiple_of(i * piece, piece), piece)
        out[here, :] = (updated[here, :] * inverse).astype(jnp.bfloat16)
        return 0

    lax.fori_loop(0, count, divide, 0)


def updated_modes(planes, base, basis_modes, low, turned, scale, rate, coord_count):
    n, pair = lax.axis_size("patch"), lax.axis_size("batch")
    coords, subjects, verts = planes.shape
    width = basis_modes.shape[2]
    rows = coords * verts
    tile = math.gcd(verts, 512)
    tiles = rows // tile
    return pl.pallas_call(
        functools.partial(update_kernel, scale, rate, coord_count),
        out_shape=(
            jax.ShapeDtypeStruct((rows, width), jnp.bfloat16),
            jax.ShapeDtypeStruct((1, width), jnp.float32),
        ),
        in_specs=[ANY, ANY, VMEM, VMEM, VMEM],
        out_specs=(VMEM, VMEM),
        scratch_shapes=[
            pltpu.VMEM((tiles, subjects, tile), jnp.bfloat16),
            pltpu.VMEM((rows, width), jnp.float32),
            pltpu.VMEM((pair, rows, width), jnp.bfloat16),
            pltpu.VMEM((n, 8, width), jnp.float32),
            pltpu.SemaphoreType.DMA((tiles + 1,)),
            pltpu.SemaphoreType.DMA((pair, tiles)),
            pltpu.SemaphoreType.DMA((pair, tiles)),
            pltpu.SemaphoreType.DMA((n,)),
            pltpu.SemaphoreType.DMA((n,)),
        ],
        compiler_params=pltpu.CompilerParams(
            collective_id=1, has_side_effects=True, vmem_limit_bytes=LIMIT
        ),
        name="update",
    )(planes, base.reshape(rows, width), basis_modes, low, turned)


def body(subjects, basis_modes, laplace_blocks, columns):
    subject_count, coords, vert_count = subjects.shape
    mode_count = basis_modes.shape[2]
    batch = lax.axis_size("batch")
    coord_count = coords * vert_count * lax.axis_size("patch")
    scale_inv = 1.0 / math.sqrt(coord_count)
    planes = subjects.transpose(1, 0, 2)
    partial_value = lax.dot_general(
        subjects, basis_modes, (((1, 2), (0, 1)), ((), ())), preferred_element_type=jnp.float32
    )
    scores, low, turned, *edges = reduce_scores(
        partial_value, basis_modes, laplace_blocks, columns, scale_inv
    )
    base = smoothed(basis_modes, laplace_blocks, columns, *edges)
    rate = 4.0 / (subject_count * batch)
    new_modes, norms = updated_modes(
        planes, base, basis_modes, low, turned, scale_inv, rate, coord_count
    )
    return (scores, new_modes.reshape(coords, vert_count, mode_count), norms.reshape(mode_count))


def solution(mesh):
    placed = (
        P(("groups", "batch"), None, "patch"),
        P(None, ("groups", "patch"), None),
        P("patch", None, None, None),
        P("patch", None),
    )
    return jax.shard_map(
        body,
        mesh=mesh,
        in_specs=placed,
        out_specs=(P(("groups", "batch"), None), P(None, ("groups", "patch"), None), P("groups")),
        check_vma=False,
    )
```

time: 108 us -> 77.9 us (0.72)
  starting transfers between devices: 11.2 us -> 0 us
  waiting for transfers between devices: 7.4 us -> 0 us
  Pallas kernels: 70 us -> 63.5 us
  local copies, waits for them, and re-layouts: 10.6 us -> 4.94 us
    ppermute x5 -> x0, starting transfers between devices: 11.2 us -> none  [the longest x4 11.2 us: shifted(): lax.ppermute(value, axis, [(source, source + steps) for source in range(i...]
    ppermute x5 -> x0, waiting for transfers between devices: 7.4 us -> none  [the longest x4 7.4 us: shifted(): lax.ppermute(value, axis, [(source, source + steps) for source in range(i...]
    pallas_call x1, Pallas kernels: 20.3 us -> 13.5 us  [smoothed(): pl.pallas_call(smooth_kernel, out_shape=jax.ShapeDtypeStruct((coords, ver...]
    slice x3 -> x0, local copies, waits for them, and re-layouts: 2.04 us -> none  [the longest x1 1.06 us: smoothed(): before = shifted(basis_modes[:, verts - reach:], 'patch', 1)]
    unnamed x18 -> x10, local copies, waits for them, and re-layouts: 6.89 us -> 4.94 us
    pallas_call x1 -> x0, local copies, waits for them, and re-layouts: 1.67 us -> none  [reduce_scores(): pl.pallas_call(functools.partial(sum_kernel, n, scale), out_shape=(jax.Sh...]
    pallas_call x3 -> x2, Pallas kernels: 49.7 us -> 50 us  [the longest x1 28.8 us: reduce_scores(): pl.pallas_call(functools.partial(sum_kernel, n, scale, reach), out_shape=...]
  transfers between devices with their start and end apart: 5 -> 0, of which waited for: 1 -> 0; matrix products, arithmetic and copies ran while one was open for 3% -> 0% of each run, Pallas kernels for 19% -> 0%
where the time goes in v2:
time: 77.9 us; the launch traced here: 77.6 us
  Pallas kernels  63.5 us (82%)
  matrix products  6.67 us (9%)
  local copies, waits for them, and re-layouts  4.94 us (6%)
  other arithmetic  1.88 us (2%)
    pallas_call x1, Pallas kernels, reduce_scores(): pl.pallas_call(functools.partial(sum_kernel, n, scale, reach), out_shape=...  28.8 us
    pallas_call x1, Pallas kernels, updated_modes(): pl.pallas_call(functools.partial(update_kernel, scale, rate, coord_count)...  21.2 us
    pallas_call x1, Pallas kernels, smoothed(): pl.pallas_call(smooth_kernel, out_shape=jax.ShapeDtypeStruct((coords, ver...  13.5 us
    dot_general x1, matrix products, body(): lax.dot_general(subjects, basis_modes, (((1, 2), (0, 1)), ((), ())), pref...  6.67 us
    unnamed x10, local copies, waits for them, and re-layouts  4.94 us

profile of v2, /device:TPU:0, one launch (start us, length us, event | category | flops | bytes accessed | tf_op | source)
XLA Modules:
  0.0 77.6 jit_solution(3300773134248877104)
XLA Ops:
  0.6 0.8 copy.9.columns
  1.4 0.0 copy-start.1
  1.4 0.6 broadcast_subtract_fusion.cols
  2.0 6.7 %convolution_bitcast_fusion.part_ref = f32[512,128]{1,0:T(8,128)} fusion(bf16[512,3,2560]{2,0,1:T(8,128)(2,1)} %param.4, bf16[3,2560,128]{2,1,0:T(8,128)(2,1)} %modes.5), kind=kOutput, calls=%fused_computation | convolution fusion | flops 1006632960 | bytes 10092544 | tf_op jit(solution)/shard_map/dot_general | solution.py:322
  8.7 0.0 copy-done.1
  8.7 28.8 %reduce_scores.1 = (f32[512,128]{1,0:T(8,128)}, bf16[512,128]{1,0:T(8,128)(2,1)}, bf16[128,512]{1,0:T(8,128)(2,1)}, bf16[3,256,128]{2,1,0:T(8,128)(2,1)}, bf16[3...) custom-call(f32[512,128]{1,0:T(8,128)} %convolution_bitcast_fusion.part_ref, ...), custom_call_target="tpu_custom_call" | custom-call | tf_op jit(solution)/shard_map/reduce_scores/pallas_call | solution.py:94
  37.5 1.3 %and_select_fusion.back_cols = s32[4,4]{1,0:T(4,128)} fusion(s32[40,4]{1,0:T(8,128)} %get-tuple-element.13, s32[]{:T(128)S(6)} %mul.3), kind=kLoop, calls=%fused_computation.3 | loop fusion | flops 80 | bytes 132 | tf_op jit(solution)/shard_map/jit(_where)/select_n | solution.py:183
  38.8 13.5 %smooth.1 = f32[3,2560,128]{2,1,0:T(8,128)} custom-call(s32[40,4]{1,0:T(8,128)} %broadcast_subtract_fusion.cols, s32[4,4]{1,0:T(4,128)} %and_select_fusion.back_cols, bf16[40,4,64,64]{3,2,1,0:T(8,128)(2,1)} %blocks.3, bf16[4,4,64,64]{3,2,1,0:T(8,128)(2,1)} %get-tuple-element.14.back_blocks, bf16[3,2560,128]{2,1,0:T(8,128)(2,1)} %modes.5, ...), custom_call_target="tpu_custom_call" | custom-call | tf_op jit(solution)/shard_map/smooth/pallas_call | solution.py:184
  52.2 0.0 copy-start
  52.2 21.2 %update.1 = (bf16[7680,128]{1,0:T(8,128)(2,1)}, f32[1,128]{1,0:T(1,128)}) custom-call(bf16[3,512,2560]{2,1,0:T(8,128)(2,1)} %bitcast.9, f32[7680,128]{1,0:T(8,128)} %bitcast.8, bf16[3,2560,128]{2,1,0:T(8,128)(2,1)} %modes.5, bf16[512,128]{1,0:T(8,128)(2,1)} %get-tuple-element.17.low, bf16[128,512]{1,0:T(8,128)(2,1)} %get-tuple-element.18.turned), custom_call_target="tpu_custom_call" | custom-call | tf_op jit(solution)/shard_map/update/pallas_call | solution.py:289
  73.4 0.0 copy-start.2
  73.4 0.0 copy-done
  73.5 0.7 copy.15
  74.2 2.9 %copy.16 = bf16[3,2560,128]{2,1,0:T(8,128)(2,1)} copy(bf16[3,2560,128]{2,1,0:T(8,128)(2,1)} %bitcast.10) | data formatting | bytes 3932160
  77.1 0.0 copy-done.2
  77.1 0.5 copy.17
Async XLA Ops:
  1.4 7.3 %copy-start.1 = (s32[40,4]{1,0:T(8,128)}, s32[40,4]{1,0:T(8,128)S(1)}, u32[]{:S(2)}) copy-start(s32[40,4]{1,0:T(8,128)S(1)} %copy.9.columns) | copy-start | bytes 1924
  52.2 21.2 %copy-start = (f32[512,128]{1,0:T(8,128)S(1)}, f32[512,128]{1,0:T(8,128)}, u32[]{:S(2)}) copy-start(f32[512,128]{1,0:T(8,128)} %get-tuple-element.24) | copy-start | bytes 786436
  73.4 3.7 %copy-start.2 = (f32[1,128]{1,0:T(1,128)S(1)}, f32[1,128]{1,0:T(1,128)}, u32[]{:S(2)}) copy-start(f32[1,128]{1,0:T(1,128)} %get-tuple-element.20) | copy-start | bytes 1540

commit v3 on v2

--- a/solution.py
+++ b/solution.py
@@ -30,8 +30,8 @@
 
 
 def sum_kernel(
-    n, scale, reach, part_ref, modes, blocks, columns, out_ref, low_ref, turned_ref,
-    after, before, back_blocks, back_cols, land, full, send_a, recv_a, send_b, recv_b, send_c, recv_c,
+    n, scale, part_ref, modes, out_ref, low_ref, turned_ref, after,
+    land, full, send_a, recv_a, send_b, recv_b, send_c, recv_c,
 ):
     greet(("patch",))
     me = lax.axis_index("patch")
@@ -54,16 +54,23 @@
         to = lax.rem(me + step, n)
         source = part_ref.at[pl.ds(pl.multiple_of(to * rows, rows), rows)]
         copies.append(start(source, land.at[step], to, send_a.at[step], recv_a.at[step]))
-    following, previous = lax.rem(me + 1, n), lax.rem(me + n - 1, n)
-    verts, count = modes.shape[1], blocks.shape[0]
-    edges = []
-    for index, (source, target, to) in enumerate((
-        (blocks.at[pl.ds(count - GHOST, GHOST)], back_blocks, following),
-        (columns, back_cols, following),
-        (modes.at[:, pl.ds(verts - reach, reach)], before, following),
-        (modes.at[:, pl.ds(0, reach)], after, previous),
-    )):
-        edges.append(start(source, target, to, send_c.at[index], recv_c.at[index]))
+    edge = pltpu.make_async_remote_copy(
+        src_ref=modes.at[:, pl.ds(0, after.shape[1])],
+        dst_ref=after,
+        send_sem=send_c,
+        recv_sem=recv_c,
+        device_id={"patch": lax.rem(me + n - 1, n)},
+        device_id_type=MESH,
+    )
+
+    @pl.when(me > 0)
+    def _():
+        edge.start()
+
+    @pl.when(me == n - 1)
+    def _():
+        after[...] = jnp.zeros_like(after)
+
     own = pl.ds(pl.multiple_of(me * rows, rows), rows)
     total = part_ref[own, :]
     for step, copy in enumerate(copies, 1):
@@ -80,48 +87,47 @@
     out_ref[...] = scores
     low_ref[...] = full[...]
     turned_ref[...] = scores.T.astype(jnp.bfloat16)
-    for copy in edges:
-        copy.wait()
-
-
-def reduce_scores(partial_value, basis_modes, laplace_blocks, columns, scale):
+
+    @pl.when(me > 0)
+    def _():
+        edge.wait_send()
+
+    @pl.when(me < n - 1)
+    def _():
+        edge.wait_recv()
+
+
+def reduce_scores(partial_value, basis_modes, reach, scale):
     n = lax.axis_size("patch")
     rows, width = partial_value.shape
     coords = basis_modes.shape[0]
-    per_row, side = laplace_blocks.shape[1:3]
-    reach = GHOST * side
     chunk = pltpu.VMEM((n, rows // n, width), jnp.float32)
     return pl.pallas_call(
-        functools.partial(sum_kernel, n, scale, reach),
+        functools.partial(sum_kernel, n, scale),
         out_shape=(
             jax.ShapeDtypeStruct((rows, width), jnp.float32),
             jax.ShapeDtypeStruct((rows, width), jnp.bfloat16),
             jax.ShapeDtypeStruct((width, rows), jnp.bfloat16),
             jax.ShapeDtypeStruct((coords, reach, width), jnp.bfloat16),
-            jax.ShapeDtypeStruct((coords, reach, width), jnp.bfloat16),
-            jax.ShapeDtypeStruct((GHOST, per_row, side, side), jnp.bfloat16),
-            jax.ShapeDtypeStruct(columns.shape, columns.dtype),
         ),
-        in_specs=[VMEM, ANY, ANY, VMEM],
-        out_specs=(VMEM, VMEM, VMEM, ANY, ANY, ANY, VMEM),
+        in_specs=[VMEM, ANY],
+        out_specs=(VMEM,) * 4,
         scratch_shapes=[chunk, pltpu.VMEM((rows, width), jnp.bfloat16)]
         + [pltpu.SemaphoreType.DMA((n,))] * 4
-        + [pltpu.SemaphoreType.DMA((4,))] * 2,
+        + [pltpu.SemaphoreType.DMA] * 2,
         compiler_params=pltpu.CompilerParams(collective_id=0, has_side_effects=True),
         name="reduce_scores",
-    )(partial_value, basis_modes, laplace_blocks, columns)
-
-
-def smooth_kernel(cols, back_cols, blocks, back_blocks, modes, after, before, out, wide, acc):
+    )(partial_value, basis_modes)
+
+
+def smooth_kernel(cols, blocks, modes, after, out, carry, wide, acc):
     count, per_row, side, _ = blocks.shape
     coords, verts, width = modes.shape
-    reach = after.shape[1]
     ones = jnp.ones((wide.shape[0], width), jnp.bfloat16)
     for c in range(coords):
         lanes = slice(c * width, (c + 1) * width)
         wide[:verts, lanes] = modes[c]
-        wide[verts : verts + reach, lanes] = after[c]
-        wide[verts + reach :, lanes] = before[c]
+        wide[verts:, lanes] = after[c]
     wide[:, coords * width :] = ones
     acc[...] = jnp.zeros_like(acc)
 
@@ -152,13 +158,7 @@
 
     lax.fori_loop(0, count // group, step, 0)
 
-    def back_step(i, _):
-        joined = jnp.concatenate([back_blocks[i, slot] for slot in range(per_row)], axis=1)
-        targets = [back_cols[i, slot] for slot in range(per_row)]
-        scatter(joined, count + reach // side + i, targets)
-        return 0
-
-    lax.fori_loop(0, back_blocks.shape[0], back_step, 0)
+    carry[...] = acc[verts:, :].astype(jnp.bfloat16)
 
     def finish(i, _):
         rows = rows_of(i)
@@ -173,31 +173,32 @@
     lax.fori_loop(0, count, finish, 0)
 
 
-def smoothed(basis_modes, laplace_blocks, columns, after, before, back_blocks, back_cols):
+def smoothed(basis_modes, laplace_blocks, columns, after):
     count, per_row, side, _ = laplace_blocks.shape
     coords, verts, width = basis_modes.shape
-    first = lax.axis_index("patch") * count
-    total = count + 2 * GHOST
-    cols = columns - first
-    back = back_cols[count - GHOST :] - first
-    back = jnp.where((back >= 0) & (back < GHOST), back, total - 1)
+    cols = columns - lax.axis_index("patch") * count
+    reach = after.shape[1]
+    lanes = (coords + 1) * width
     return pl.pallas_call(
         smooth_kernel,
-        out_shape=jax.ShapeDtypeStruct((coords, verts, width), jnp.float32),
-        in_specs=[SMEM, SMEM] + [VMEM] * 5,
-        out_specs=VMEM,
+        out_shape=(
+            jax.ShapeDtypeStruct((coords, verts, width), jnp.float32),
+            jax.ShapeDtypeStruct((reach, lanes), jnp.bfloat16),
+        ),
+        in_specs=[SMEM] + [VMEM] * 3,
+        out_specs=(VMEM, VMEM),
         scratch_shapes=[
-            pltpu.VMEM((total * side, (coords + 1) * width), jnp.bfloat16),
-            pltpu.VMEM((total * side, (coords + 1) * width), jnp.float32),
+            pltpu.VMEM((verts + reach, lanes), jnp.bfloat16),
+            pltpu.VMEM((verts + reach, lanes), jnp.float32),
         ],
         compiler_params=pltpu.CompilerParams(vmem_limit_bytes=LIMIT),
         name="smooth",
-    )(cols, back, laplace_blocks, back_blocks, basis_modes, after, before)
+    )(cols, laplace_blocks, basis_modes, after)
 
 
 def update_kernel(
-    scale, rate, coord_count, planes, base, modes, low, turned, out, norms,
-    held, updated, both, slots, load, send_h, recv_h, send_n, recv_n,
+    scale, rate, coord_count, planes, base, modes, low, turned, carry, out, norms,
+    held, updated, both, slots, extra, load, send_h, recv_h, send_n, recv_n, send_c, recv_c,
 ):
     n, me = lax.axis_size("patch"), lax.axis_index("patch")
     pair, half = lax.axis_size("batch"), lax.axis_index("batch")
@@ -212,6 +213,22 @@
     loads.append(pltpu.make_async_copy(base, updated, load.at[tiles]))
     loads[-1].start()
     greet(("patch", "batch"))
+    edge = pltpu.make_async_remote_copy(
+        src_ref=carry,
+        dst_ref=extra,
+        send_sem=send_c,
+        recv_sem=recv_c,
+        device_id={"patch": lax.rem(me + 1, n)},
+        device_id_type=MESH,
+    )
+
+    @pl.when(me < n - 1)
+    def _():
+        edge.start()
+
+    @pl.when(me == 0)
+    def _():
+        extra[...] = jnp.zeros_like(extra)
 
     copies = []
     for i in range(tiles):
@@ -235,9 +252,24 @@
             )
             copy.start()
             copies.append(copy)
+    loads[tiles].wait()
+
+    @pl.when(me < n - 1)
+    def _():
+        edge.wait_send()
+
+    @pl.when(me > 0)
+    def _():
+        edge.wait_recv()
+
+    reach = extra.shape[0]
+    degree = extra[:, coords * width :].astype(jnp.float32)
+    for c in range(coords):
+        mode = modes[c, :reach, :].astype(jnp.float32)
+        terms = degree * mode - extra[:, c * width : (c + 1) * width].astype(jnp.float32)
+        updated[c * verts : c * verts + reach, :] += -0.2 * terms
     for copy in copies:
         copy.wait()
-    loads[tiles].wait()
 
     piece = math.gcd(coords * verts, 256)
 
@@ -279,7 +311,7 @@
     lax.fori_loop(0, count, divide, 0)
 
 
-def updated_modes(planes, base, basis_modes, low, turned, scale, rate, coord_count):
+def updated_modes(planes, base, carry, basis_modes, low, turned, scale, rate, coord_count):
     n, pair = lax.axis_size("patch"), lax.axis_size("batch")
     coords, subjects, verts = planes.shape
     width = basis_modes.shape[2]
@@ -292,24 +324,27 @@
             jax.ShapeDtypeStruct((rows, width), jnp.bfloat16),
             jax.ShapeDtypeStruct((1, width), jnp.float32),
         ),
-        in_specs=[ANY, ANY, VMEM, VMEM, VMEM],
+        in_specs=[ANY, ANY] + [VMEM] * 4,
         out_specs=(VMEM, VMEM),
         scratch_shapes=[
             pltpu.VMEM((tiles, subjects, tile), jnp.bfloat16),
             pltpu.VMEM((rows, width), jnp.float32),
             pltpu.VMEM((pair, rows, width), jnp.bfloat16),
             pltpu.VMEM((n, 8, width), jnp.float32),
+            pltpu.VMEM(carry.shape, carry.dtype),
             pltpu.SemaphoreType.DMA((tiles + 1,)),
             pltpu.SemaphoreType.DMA((pair, tiles)),
             pltpu.SemaphoreType.DMA((pair, tiles)),
             pltpu.SemaphoreType.DMA((n,)),
             pltpu.SemaphoreType.DMA((n,)),
+            pltpu.SemaphoreType.DMA,
+            pltpu.SemaphoreType.DMA,
         ],
         compiler_params=pltpu.CompilerParams(
             collective_id=1, has_side_effects=True, vmem_limit_bytes=LIMIT
         ),
         name="update",
-    )(planes, base.reshape(rows, width), basis_modes, low, turned)
+    )(planes, base.reshape(rows, width), basis_modes, low, turned, carry)
 
 
 def body(subjects, basis_modes, laplace_blocks, columns):
@@ -322,13 +357,12 @@
     partial_value = lax.dot_general(
         subjects, basis_modes, (((1, 2), (0, 1)), ((), ())), preferred_element_type=jnp.float32
     )
-    scores, low, turned, *edges = reduce_scores(
-        partial_value, basis_modes, laplace_blocks, columns, scale_inv
-    )
-    base = smoothed(basis_modes, laplace_blocks, columns, *edges)
+    reach = GHOST * laplace_blocks.shape[2]
+    scores, low, turned, after = reduce_scores(partial_value, basis_modes, reach, scale_inv)
+    base, carry = smoothed(basis_modes, laplace_blocks, columns, after)
     rate = 4.0 / (subject_count * batch)
     new_modes, norms = updated_modes(
-        planes, base, basis_modes, low, turned, scale_inv, rate, coord_count
+        planes, base, carry, basis_modes, low, turned, scale_inv, rate, coord_count
     )
     return (scores, new_modes.reshape(coords, vert_count, mode_count), norms.reshape(mode_count))
 

time: 77.9 us -> 67.8 us (0.87)
  Pallas kernels: 63.5 us -> 54.6 us
  other arithmetic: 1.88 us -> 0.61 us
    pallas_call x2, Pallas kernels: 42.3 us -> 33.1 us  [the longest x1 21.1 us: reduce_scores(): pl.pallas_call(functools.partial(sum_kernel, n, scale), out_shape=(jax.Sh...]
    select_n x1 -> x0, other arithmetic: 1.26 us -> none  [smoothed(): back = jnp.where((back >= 0) & (back < GHOST), back, total - 1)]
    unnamed x10 -> x8, local copies, waits for them, and re-layouts: 4.94 us -> 4.93 us
where the time goes in v3:
time: 67.8 us; the launch traced here: 67.5 us
  Pallas kernels  54.6 us (81%)
  matrix products  6.67 us (10%)
  local copies, waits for them, and re-layouts  4.93 us (7%)
    pallas_call x1, Pallas kernels, updated_modes(): pl.pallas_call(functools.partial(update_kernel, scale, rate, coord_count)...  21.6 us
    pallas_call x1, Pallas kernels, reduce_scores(): pl.pallas_call(functools.partial(sum_kernel, n, scale), out_shape=(jax.Sh...  21.1 us
    pallas_call x1, Pallas kernels, smoothed(): pl.pallas_call(smooth_kernel, out_shape=(jax.ShapeDtypeStruct((coords, ve...  12 us
    dot_general x1, matrix products, body(): lax.dot_general(subjects, basis_modes, (((1, 2), (0, 1)), ((), ())), pref...  6.67 us
    unnamed x8, local copies, waits for them, and re-layouts  4.93 us

profile of v3, /device:TPU:0, one launch (start us, length us, event | category | flops | bytes accessed | tf_op | source)
XLA Modules:
  0.0 67.5 jit_solution(13506554734967887247)
XLA Ops:
  0.6 0.8 %copy.8 = s32[40,4]{1,0:T(8,128)S(1)} copy(s32[40,4]{0,1:T(4,128)} %param.7) | data formatting | bytes 1280 | tf_op args[3]
  1.4 0.6 broadcast_subtract_fusion.cols
  2.0 6.7 %convolution_bitcast_fusion.part_ref = f32[512,128]{1,0:T(8,128)} fusion(bf16[512,3,2560]{2,0,1:T(8,128)(2,1)} %param.4, bf16[3,2560,128]{2,1,0:T(8,128)(2,1)} %modes.5), kind=kOutput, calls=%fused_computation | convolution fusion | flops 1006632960 | bytes 10092544 | tf_op jit(solution)/shard_map/dot_general | solution.py:357
  8.7 21.1 %reduce_scores.1 = (f32[512,128]{1,0:T(8,128)}, bf16[512,128]{1,0:T(8,128)(2,1)}, bf16[128,512]{1,0:T(8,128)(2,1)}, bf16[3,256,128]{2,1,0:T(8,128)(2,1)}) custom-call(f32[512,128]{1,0:T(8,128)} %convolution_bitcast_fusion.part_ref, bf16[3,2560,128]{2,1,0:T(8,128)(2,1)} %modes.5), custom_call_target="tpu_custom_call" | custom-call | tf_op jit(solution)/shard_map/reduce_scores/pallas_call | solution.py:105
  29.8 12.0 %smooth.1 = (f32[3,2560,128]{2,1,0:T(8,128)}, bf16[256,512]{1,0:T(8,128)(2,1)}) custom-call(s32[40,4]{1,0:T(8,128)} %broadcast_subtract_fusion.cols, bf16[40,4,64,64]{3,2,1,0:T(8,128)(2,1)} %blocks.1, bf16[3,2560,128]{2,1,0:T(8,128)(2,1)} %modes.5, bf16[3,256,128]{2,1,0:T(8,128)(2,1)} %get-tuple-element.12.after), custom_call_target="tpu_custom_call" | custom-call | tf_op jit(solution)/shard_map/smooth/pallas_call | solution.py:182
  41.7 0.0 copy-start
  41.8 21.6 %update.1 = (bf16[7680,128]{1,0:T(8,128)(2,1)}, f32[1,128]{1,0:T(1,128)}) custom-call(bf16[3,512,2560]{2,1,0:T(8,128)(2,1)} %bitcast.8, f32[7680,128]{1,0:T(8,128)} %bitcast.9, bf16[3,2560,128]{2,1,0:T(8,128)(2,1)} %modes.5, bf16[512,128]{1,0:T(8,128)(2,1)} %get-tuple-element.14.low, bf16[128,512]{1,0:T(8,128)(2,1)} %get-tuple-element.15.turned, ...), custom_call_target="tpu_custom_call" | custom-call | tf_op jit(solution)/shard_map/update/pallas_call | solution.py:321
  63.3 0.0 copy-start.1
  63.3 0.0 copy-done
  63.3 0.7 %copy.13 = f32[512,128]{1,0:T(8,128)} copy(f32[512,128]{1,0:T(8,128)S(1)} %copy-done) | data formatting | bytes 524288
  64.1 2.9 %copy.14 = bf16[3,2560,128]{2,1,0:T(8,128)(2,1)} copy(bf16[3,2560,128]{2,1,0:T(8,128)(2,1)} %bitcast.10) | data formatting | bytes 3932160
  67.0 0.0 copy-done.1
  67.0 0.5 copy.15
Async XLA Ops:
  41.7 21.6 %copy-start = (f32[512,128]{1,0:T(8,128)S(1)}, f32[512,128]{1,0:T(8,128)}, u32[]{:S(2)}) copy-start(f32[512,128]{1,0:T(8,128)} %get-tuple-element.22) | copy-start | bytes 786436
  63.3 3.7 %copy-start.1 = (f32[1,128]{1,0:T(1,128)S(1)}, f32[1,128]{1,0:T(1,128)}, u32[]{:S(2)}) copy-start(f32[1,128]{1,0:T(1,128)} %get-tuple-element.18) | copy-start | bytes 1540

commit v4 on v3

--- a/solution.py
+++ b/solution.py
@@ -30,7 +30,7 @@
 
 
 def sum_kernel(
-    n, scale, part_ref, modes, out_ref, low_ref, turned_ref, after,
+    n, scale, part_ref, modes, low_ref, turned_ref, after,
     land, full, send_a, recv_a, send_b, recv_b, send_c, recv_c,
 ):
     greet(("patch",))
@@ -83,10 +83,8 @@
         copies.append(start(full.at[own], full.at[own], to, send_b.at[step], recv_b.at[step]))
     for copy in copies:
         copy.wait()
-    scores = full[...].astype(jnp.float32)
-    out_ref[...] = scores
     low_ref[...] = full[...]
-    turned_ref[...] = scores.T.astype(jnp.bfloat16)
+    turned_ref[...] = full[...].astype(jnp.float32).T.astype(jnp.bfloat16)
 
     @pl.when(me > 0)
     def _():
@@ -105,13 +103,12 @@
     return pl.pallas_call(
         functools.partial(sum_kernel, n, scale),
         out_shape=(
-            jax.ShapeDtypeStruct((rows, width), jnp.float32),
             jax.ShapeDtypeStruct((rows, width), jnp.bfloat16),
             jax.ShapeDtypeStruct((width, rows), jnp.bfloat16),
             jax.ShapeDtypeStruct((coords, reach, width), jnp.bfloat16),
         ),
         in_specs=[VMEM, ANY],
-        out_specs=(VMEM,) * 4,
+        out_specs=(VMEM,) * 3,
         scratch_shapes=[chunk, pltpu.VMEM((rows, width), jnp.bfloat16)]
         + [pltpu.SemaphoreType.DMA((n,))] * 4
         + [pltpu.SemaphoreType.DMA] * 2,
@@ -120,9 +117,11 @@
     )(partial_value, basis_modes)
 
 
-def smooth_kernel(cols, blocks, modes, after, out, carry, wide, acc):
+def smooth_kernel(cols, blocks, modes, after, low, out, carry, scores, wide, acc):
     count, per_row, side, _ = blocks.shape
     coords, verts, width = modes.shape
+    first = lax.axis_index("patch") * count
+    scores[...] = low[...].astype(jnp.float32)
     ones = jnp.ones((wide.shape[0], width), jnp.bfloat16)
     for c in range(coords):
         lanes = slice(c * width, (c + 1) * width)
@@ -150,7 +149,7 @@
         for inner in range(group):
             i = outer * group + inner
             joined = jnp.concatenate([blocks[i, slot] for slot in range(per_row)], axis=1)
-            targets = [cols[i, slot] for slot in range(per_row)]
+            targets = [cols[slot, i] - first for slot in range(per_row)]
             picked = jnp.concatenate([wide[rows_of(t), :] for t in targets], axis=0)
             acc[rows_of(i), :] += jnp.dot(joined, picked, preferred_element_type=jnp.float32)
             scatter(joined, i, targets)
@@ -173,10 +172,9 @@
     lax.fori_loop(0, count, finish, 0)
 
 
-def smoothed(basis_modes, laplace_blocks, columns, after):
+def smoothed(basis_modes, laplace_blocks, columns, after, low):
     count, per_row, side, _ = laplace_blocks.shape
     coords, verts, width = basis_modes.shape
-    cols = columns - lax.axis_index("patch") * count
     reach = after.shape[1]
     lanes = (coords + 1) * width
     return pl.pallas_call(
@@ -184,16 +182,17 @@
         out_shape=(
             jax.ShapeDtypeStruct((coords, verts, width), jnp.float32),
             jax.ShapeDtypeStruct((reach, lanes), jnp.bfloat16),
+            jax.ShapeDtypeStruct(low.shape, jnp.float32),
         ),
-        in_specs=[SMEM] + [VMEM] * 3,
-        out_specs=(VMEM, VMEM),
+        in_specs=[SMEM] + [VMEM] * 4,
+        out_specs=(VMEM,) * 3,
         scratch_shapes=[
             pltpu.VMEM((verts + reach, lanes), jnp.bfloat16),
             pltpu.VMEM((verts + reach, lanes), jnp.float32),
         ],
         compiler_params=pltpu.CompilerParams(vmem_limit_bytes=LIMIT),
         name="smooth",
-    )(cols, laplace_blocks, basis_modes, after)
+    )(columns.T, laplace_blocks, basis_modes, after, low)
 
 
 def update_kernel(
@@ -230,28 +229,34 @@
     def _():
         extra[...] = jnp.zeros_like(extra)
 
-    copies = []
-    for i in range(tiles):
+    def residual_of(i):
         mode = modes[i // per, (i % per) * tile : (i % per + 1) * tile, :]
-        loads[i].wait()
         recon = lax.dot_general(
             low[...], mode, (((1,), (1,)), ((), ())), preferred_element_type=jnp.float32
         )
-        residual = (held[i].astype(jnp.float32) - recon * scale).astype(jnp.bfloat16)
-        hebb = jnp.dot(turned[...], residual, preferred_element_type=jnp.float32)
-        rows = pl.ds(i * tile, tile)
-        both[half, rows, :] = hebb.T.astype(jnp.bfloat16)
-        for step in range(1, pair):
-            copy = pltpu.make_async_remote_copy(
-                src_ref=both.at[half, rows],
-                dst_ref=both.at[half, rows],
-                send_sem=send_h.at[step, i],
-                recv_sem=recv_h.at[step, i],
-                device_id={"batch": lax.rem(half + step, pair)},
-                device_id_type=MESH,
-            )
-            copy.start()
-            copies.append(copy)
+        return (held[i].astype(jnp.float32) - recon * scale).astype(jnp.bfloat16)
+
+    copies, ready = [], None
+    for i in range(tiles + 1):
+        if i < tiles:
+            loads[i].wait()
+            residual = residual_of(i)
+        if i > 0:
+            hebb = jnp.dot(turned[...], ready, preferred_element_type=jnp.float32)
+            rows = pl.ds((i - 1) * tile, tile)
+            both[half, rows, :] = hebb.T.astype(jnp.bfloat16)
+            for step in range(1, pair):
+                copy = pltpu.make_async_remote_copy(
+                    src_ref=both.at[half, rows],
+                    dst_ref=both.at[half, rows],
+                    send_sem=send_h.at[step, i - 1],
+                    recv_sem=recv_h.at[step, i - 1],
+                    device_id={"batch": lax.rem(half + step, pair)},
+                    device_id_type=MESH,
+                )
+                copy.start()
+                copies.append(copy)
+        ready = residual
     loads[tiles].wait()
 
     @pl.when(me < n - 1)
@@ -358,8 +363,8 @@
         subjects, basis_modes, (((1, 2), (0, 1)), ((), ())), preferred_element_type=jnp.float32
     )
     reach = GHOST * laplace_blocks.shape[2]
-    scores, low, turned, after = reduce_scores(partial_value, basis_modes, reach, scale_inv)
-    base, carry = smoothed(basis_modes, laplace_blocks, columns, after)
+    low, turned, after = reduce_scores(partial_value, basis_modes, reach, scale_inv)
+    base, carry, scores = smoothed(basis_modes, laplace_blocks, columns, after, low)
     rate = 4.0 / (subject_count * batch)
     new_modes, norms = updated_modes(
         planes, base, carry, basis_modes, low, turned, scale_inv, rate, coord_count

time: 67.8 us -> 64.1 us (0.945)
  Pallas kernels: 54.6 us -> 53.1 us
  local copies, waits for them, and re-layouts: 4.93 us -> 3.46 us
    pallas_call x1, Pallas kernels: 21.6 us -> 20 us  [updated_modes(): pl.pallas_call(functools.partial(update_kernel, scale, rate, coord_count)...]
    unnamed x8 -> x4, local copies, waits for them, and re-layouts: 4.93 us -> 3.46 us
where the time goes in v4:
time: 64.1 us; the launch traced here: 63.9 us
  Pallas kernels  53.1 us (83%)
  matrix products  6.68 us (10%)
  local copies, waits for them, and re-layouts  3.46 us (5%)
  between operations  0.66 us (1%)
    pallas_call x1, Pallas kernels, reduce_scores(): pl.pallas_call(functools.partial(sum_kernel, n, scale), out_shape=(jax.Sh...  21 us
    pallas_call x1, Pallas kernels, updated_modes(): pl.pallas_call(functools.partial(update_kernel, scale, rate, coord_count)...  20 us
    pallas_call x1, Pallas kernels, smoothed(): pl.pallas_call(smooth_kernel, out_shape=(jax.ShapeDtypeStruct((coords, ve...  12.1 us
    dot_general x1, matrix products, body(): lax.dot_general(subjects, basis_modes, (((1, 2), (0, 1)), ((), ())), pref...  6.68 us
    unnamed x4, local copies, waits for them, and re-layouts  3.46 us

profile of v4, /device:TPU:0, one launch (start us, length us, event | category | flops | bytes accessed | tf_op | source)
XLA Modules:
  0.0 63.9 jit_solution(9200744210289373346)
XLA Ops:
  0.6 6.7 %convolution_bitcast_fusion.part_ref = f32[512,128]{1,0:T(8,128)} fusion(bf16[512,3,2560]{2,0,1:T(8,128)(2,1)} %param.4, bf16[3,2560,128]{2,1,0:T(8,128)(2,1)} %modes.5), kind=kOutput, calls=%fused_computation | convolution fusion | flops 1006632960 | bytes 10092544 | tf_op jit(solution)/shard_map/dot_general | solution.py:362
  7.3 21.0 %reduce_scores.1 = (bf16[512,128]{1,0:T(8,128)(2,1)}, bf16[128,512]{1,0:T(8,128)(2,1)}, bf16[3,256,128]{2,1,0:T(8,128)(2,1)}) custom-call(f32[512,128]{1,0:T(8,128)} %convolution_bitcast_fusion.part_ref, bf16[3,2560,128]{2,1,0:T(8,128)(2,1)} %modes.5), custom_call_target="tpu_custom_call" | custom-call | tf_op jit(solution)/shard_map/reduce_scores/pallas_call | solution.py:103
  28.3 12.1 %smooth.1 = (f32[3,2560,128]{2,1,0:T(8,128)}, bf16[256,512]{1,0:T(8,128)(2,1)}, f32[512,128]{1,0:T(8,128)}) custom-call(s32[4,40]{1,0:T(4,128)} %bitcast.12, bf16[40,4,64,64]{3,2,1,0:T(8,128)(2,1)} %blocks.1, bf16[3,2560,128]{2,1,0:T(8,128)(2,1)} %modes.5, bf16[3,256,128]{2,1,0:T(8,128)(2,1)} %get-tuple-element.11.after, bf16[512,128]{1,0:T(8,128)(2,1)} %get-tuple-element.12.low), custom_call_target="tpu_custom_call" | custom-call | tf_op jit(solution)/shard_map/smooth/pallas_call | solution.py:180
  40.4 20.0 %update.1 = (bf16[7680,128]{1,0:T(8,128)(2,1)}, f32[1,128]{1,0:T(1,128)}) custom-call(bf16[3,512,2560]{2,1,0:T(8,128)(2,1)} %bitcast.9, f32[7680,128]{1,0:T(8,128)} %bitcast.10, bf16[3,2560,128]{2,1,0:T(8,128)(2,1)} %modes.5, bf16[512,128]{1,0:T(8,128)(2,1)} %get-tuple-element.12.low, bf16[128,512]{1,0:T(8,128)(2,1)} %get-tuple-element.15.turned, ...), custom_call_target="tpu_custom_call" | custom-call | tf_op jit(solution)/shard_map/update/pallas_call | solution.py:326
  60.4 0.0 copy-start
  60.4 2.9 %copy.9 = bf16[3,2560,128]{2,1,0:T(8,128)(2,1)} copy(bf16[3,2560,128]{2,1,0:T(8,128)(2,1)} %bitcast.11) | data formatting | bytes 3932160
  63.4 0.0 copy-done
  63.4 0.5 copy.10
Async XLA Ops:
  60.4 3.0 %copy-start = (f32[1,128]{1,0:T(1,128)S(1)}, f32[1,128]{1,0:T(1,128)}, u32[]{:S(2)}) copy-start(f32[1,128]{1,0:T(1,128)} %get-tuple-element.18) | copy-start | bytes 1540

commit v5 on v4

--- a/solution.py
+++ b/solution.py
@@ -143,7 +143,7 @@
         for slot, target in enumerate(targets):
             acc[rows_of(target), :] += moved[slot * side : (slot + 1) * side]
 
-    group = math.gcd(count, 4)
+    group = math.gcd(count, 8)
 
     def step(outer, _):
         for inner in range(group):
@@ -321,7 +321,7 @@
     coords, subjects, verts = planes.shape
     width = basis_modes.shape[2]
     rows = coords * verts
-    tile = math.gcd(verts, 512)
+    tile = math.gcd(verts, 1280)
     tiles = rows // tile
     return pl.pallas_call(
         functools.partial(update_kernel, scale, rate, coord_count),

time: 64.1 us -> 62.2 us (0.970)
  Pallas kernels: 53.1 us -> 51.2 us
    pallas_call x1, Pallas kernels: 12.1 us -> 10.9 us  [smoothed(): pl.pallas_call(smooth_kernel, out_shape=(jax.ShapeDtypeStruct((coords, ve...]
    pallas_call x1, Pallas kernels: 20 us -> 19.3 us  [updated_modes(): pl.pallas_call(functools.partial(update_kernel, scale, rate, coord_count)...]
where the time goes in v5:
time: 62.2 us; the launch traced here: 62 us
  Pallas kernels  51.2 us (82%)
  matrix products  6.68 us (11%)
  local copies, waits for them, and re-layouts  3.46 us (6%)
  between operations  0.66 us (1%)
    pallas_call x1, Pallas kernels, reduce_scores(): pl.pallas_call(functools.partial(sum_kernel, n, scale), out_shape=(jax.Sh...  21 us
    pallas_call x1, Pallas kernels, updated_modes(): pl.pallas_call(functools.partial(update_kernel, scale, rate, coord_count)...  19.3 us
    pallas_call x1, Pallas kernels, smoothed(): pl.pallas_call(smooth_kernel, out_shape=(jax.ShapeDtypeStruct((coords, ve...  10.9 us
    dot_general x1, matrix products, body(): lax.dot_general(subjects, basis_modes, (((1, 2), (0, 1)), ((), ())), pref...  6.68 us
    unnamed x4, local copies, waits for them, and re-layouts  3.46 us

profile of v5, /device:TPU:0, one launch (start us, length us, event | category | flops | bytes accessed | tf_op | source)
XLA Modules:
  0.0 62.0 jit_solution(17659879710440556367)
XLA Ops:
  0.6 6.7 %convolution_bitcast_fusion.part_ref = f32[512,128]{1,0:T(8,128)} fusion(bf16[512,3,2560]{2,0,1:T(8,128)(2,1)} %param.4, bf16[3,2560,128]{2,1,0:T(8,128)(2,1)} %modes.5), kind=kOutput, calls=%fused_computation | convolution fusion | flops 1006632960 | bytes 10092544 | tf_op jit(solution)/shard_map/dot_general | solution.py:362
  7.3 21.0 %reduce_scores.1 = (bf16[512,128]{1,0:T(8,128)(2,1)}, bf16[128,512]{1,0:T(8,128)(2,1)}, bf16[3,256,128]{2,1,0:T(8,128)(2,1)}) custom-call(f32[512,128]{1,0:T(8,128)} %convolution_bitcast_fusion.part_ref, bf16[3,2560,128]{2,1,0:T(8,128)(2,1)} %modes.5), custom_call_target="tpu_custom_call" | custom-call | tf_op jit(solution)/shard_map/reduce_scores/pallas_call | solution.py:103
  28.3 10.9 %smooth.1 = (f32[3,2560,128]{2,1,0:T(8,128)}, bf16[256,512]{1,0:T(8,128)(2,1)}, f32[512,128]{1,0:T(8,128)}) custom-call(s32[4,40]{1,0:T(4,128)} %bitcast.12, bf16[40,4,64,64]{3,2,1,0:T(8,128)(2,1)} %blocks.1, bf16[3,2560,128]{2,1,0:T(8,128)(2,1)} %modes.5, bf16[3,256,128]{2,1,0:T(8,128)(2,1)} %get-tuple-element.11.after, bf16[512,128]{1,0:T(8,128)(2,1)} %get-tuple-element.12.low), custom_call_target="tpu_custom_call" | custom-call | tf_op jit(solution)/shard_map/smooth/pallas_call | solution.py:180
  39.2 19.3 %update.1 = (bf16[7680,128]{1,0:T(8,128)(2,1)}, f32[1,128]{1,0:T(1,128)}) custom-call(bf16[3,512,2560]{2,1,0:T(8,128)(2,1)} %bitcast.9, f32[7680,128]{1,0:T(8,128)} %bitcast.10, bf16[3,2560,128]{2,1,0:T(8,128)(2,1)} %modes.5, bf16[512,128]{1,0:T(8,128)(2,1)} %get-tuple-element.12.low, bf16[128,512]{1,0:T(8,128)(2,1)} %get-tuple-element.15.turned, ...), custom_call_target="tpu_custom_call" | custom-call | tf_op jit(solution)/shard_map/update/pallas_call | solution.py:326
  58.5 0.0 copy-start
  58.5 2.9 %copy.9 = bf16[3,2560,128]{2,1,0:T(8,128)(2,1)} copy(bf16[3,2560,128]{2,1,0:T(8,128)(2,1)} %bitcast.11) | data formatting | bytes 3932160
  61.5 0.0 copy-done
  61.5 0.5 copy.10
Async XLA Ops:
  58.5 3.0 %copy-start = (f32[1,128]{1,0:T(1,128)S(1)}, f32[1,128]{1,0:T(1,128)}, u32[]{:S(2)}) copy-start(f32[1,128]{1,0:T(1,128)} %get-tuple-element.18) | copy-start | bytes 1540
